TPU v7x, 256 devices: a whole 4x4x8 slice. The times are simulated.
256 devices in a mesh: req: 64 (over z, x, core), tp: 4 (over y).
Axes of the slice: x: 4, y: 4, z: 8, core: 2. Of those that a mesh axis runs over, the one named last changes fastest.
Arguments:
- hidden: bfloat16 [2048, 5120], P('req', 'tp'), may hold values from -8 to 8
- gain: float32 [5120], replicated, may hold values from 0.5 to 1.5
- head_weight: bfloat16 [5120, 131072], P(None, ('req', 'tp')), may hold values from -0.3 to 0.3
- token_ids: int32 [2048], P('req'), may hold values from 0 to 131071
- lengths: int32 [64], P('req'), may hold values from 1 to 32, as said below
- owner_device: int32 [64], replicated, may hold values from 0 to 63, each once
Outputs:
- logprob: float32 [2048], P('req')
- entropy: float32 [2048], P('req')
Inputs may be any that keep to these rules, and one draw needn't show every extreme that they name: `lengths`: each sequence has 1 to 32 live slots; some sequence has exactly 32. `owner_device`: A permutation of the req indices.
All inputs are finite; a program needn't handle non-finite values.
Results may differ from a plain program's by a relative error of at most 0.0041.
Values may be sent and summed in bfloat16 or wider, within the bound.
No kernel may reach another device: no remote copies, remote signals or barrier semaphores. Data moves between devices by JAX's collectives and lax.ppermute only.
A program may use at most 128 MiB of HBM per device.

v0:
```python
import functools

import jax
import jax.numpy as jnp
from jax import lax
from jax.experimental import pallas as pl
from jax.experimental.pallas import tpu as pltpu
from jax.sharding import Mesh
from jax.sharding import PartitionSpec as P


ALL = ("zh", "zl", "x", "core", "tp")
REQ = ("zh", "zl", "x", "core")
SPLIT = (2, 4, 4, 2, 4)
LANES = 128


def pairs(step, swap):
    out = []
    for z in range(8):
        for x in range(4):
            for core in range(2):
                along_z = (core == 0) != swap
                nz = (z + step) % 8 if along_z else z
                nx = x if along_z else (x + step) % 4
                out.append(((z * 4 + x) * 2 + core, (nz * 4 + nx) * 2 + core))
    return out


def send(value, step, swap):
    return lax.ppermute(value, REQ, pairs(step, swap))


def norm_kernel(eps, spot_ref, *refs):
    pieces, (gain_ref, out_ref) = refs[:-2], refs[-2:]
    width, quarters = gain_ref.shape[1] // 4, 4
    rows = pieces[0].shape[0]
    for h in range(2):
        mine = pieces[h * quarters : (h + 1) * quarters]
        at = pl.ds(pl.multiple_of(spot_ref[h] * rows, rows), rows)
        square = jnp.zeros((rows, 1), jnp.float32)
        for piece in mine:
            values = piece[:, :width].astype(jnp.float32)
            square += jnp.sum(values * values, axis=1, keepdims=True)
        scale = lax.rsqrt(square / (width * quarters) + eps)
        for q, piece in enumerate(mine):
            columns = pl.ds(pl.multiple_of(spot_ref[2 + q] * width, LANES), width)
            values = piece[:, :width].astype(jnp.float32)
            out_ref[at, columns] = (values * scale * gain_ref[:, columns]).astype(jnp.bfloat16)
        out_ref[at, quarters * width :] = mine[0][:, width:]


def norm(spots, pieces, gain):
    vmem = pl.BlockSpec(memory_space=pltpu.VMEM)
    return pl.pallas_call(
        functools.partial(norm_kernel, 1e-05),
        out_shape=jax.ShapeDtypeStruct((2 * pieces[0].shape[0], gain.shape[0] + LANES), jnp.bfloat16),
        in_specs=[pl.BlockSpec(memory_space=pltpu.SMEM)] + [vmem] * (len(pieces) + 1),
        out_specs=vmem,
        compiler_params=pltpu.CompilerParams(vmem_limit_bytes=4 << 20),
        name="norm",
    )(spots, *pieces, gain[None, :])


def score_kernel(n_parts, width, base_ref, *refs):
    parts, (w_own, w_other, out_ref, logits) = refs[:n_parts], refs[n_parts:]
    rows = parts[0].shape[0]
    cols = w_own.shape[1]
    tile = 256
    for half, w in enumerate((w_own, w_other)):

        def column_tile(n, carry, half=half, w=w):
            at = pl.multiple_of(n * tile, tile)
            lhs = jnp.concatenate([part[:, :width] for part in parts], axis=0)
            product = jnp.dot(lhs, w[:, pl.ds(at, tile)], preferred_element_type=jnp.float32)
            logits[:, pl.ds(pl.multiple_of(half * cols + n * tile, tile), tile)] = product
            return carry

        lax.fori_loop(0, cols // tile, column_tile, 0)

    lane = lax.broadcasted_iota(jnp.int32, (32, LANES), 1)
    slot = lax.broadcasted_iota(jnp.int32, (32, LANES), 0)
    column = lax.broadcasted_iota(jnp.int32, (32, 2 * cols), 1)
    vocab = jnp.where(column < cols, base_ref[0] + column, base_ref[1] + column - cols)
    digit = jnp.where(lane == 0, 4096.0, jnp.where(lane == 1, 64.0, jnp.where(lane == 2, 1.0, 0.0)))
    for i, part in enumerate(parts):

        def group(g, carry, i=i, part=part):
            row = pl.multiple_of(g * 32, 32)
            lg = logits[pl.ds(pl.multiple_of(i * rows + g * 32, 32), 32), :]
            code = part[pl.ds(row, 32), pl.ds(width, LANES)].astype(jnp.float32)
            ids = jnp.sum(code * digit, axis=1, keepdims=True).astype(jnp.int32)
            peak = jnp.max(lg, axis=1, keepdims=True)
            weight = jnp.exp(lg - peak)
            total = jnp.sum(weight, axis=1, keepdims=True)
            spread = jnp.sum(weight * lg, axis=1, keepdims=True)
            pick = jnp.sum(jnp.where(vocab == ids, lg, 0.0), axis=1, keepdims=True)
            stat = jnp.where(lane < 32, peak, jnp.where(lane < 64, total, jnp.where(lane < 96, spread, pick)))
            line = jnp.sum(jnp.where(lane % 32 == slot, stat, 0.0), axis=0, keepdims=True)
            out_ref[pl.ds(i * (rows // 32) + g, 1), :] = line
            return carry

        lax.fori_loop(0, rows // 32, group, 0)


def score(parts, w_own, w_other, bases):
    rows = parts[0].shape[0]
    n = len(parts)
    width = w_own.shape[0]
    cols = w_own.shape[1]
    vmem = pl.BlockSpec(memory_space=pltpu.VMEM)
    return pl.pallas_call(
        functools.partial(score_kernel, n, width),
        out_shape=jax.ShapeDtypeStruct((n * rows // 32, LANES), jnp.float32),
        in_specs=[pl.BlockSpec(memory_space=pltpu.SMEM)] + [vmem] * (n + 2),
        out_specs=vmem,
        scratch_shapes=[pltpu.VMEM((n * rows, 2 * cols), jnp.float32)],
        cost_estimate=pl.CostEstimate(
            flops=4 * n * rows * width * cols, bytes_accessed=n * rows * width * 2, transcendentals=2 * n * rows * cols
        ),
        compiler_params=pltpu.CompilerParams(vmem_limit_bytes=16 << 20),
        name="score",
    )(bases, *parts, w_own, w_other)


def table_kernel(place_ref, owner_ref, *refs):
    lines, (out_ref, table) = refs[:-2], refs[-2:]
    table[...] = jnp.zeros_like(table)
    at = 0
    for line in lines:
        for i in range(line.shape[0]):
            table[pl.ds(place_ref[at], 1), :] = line[i : i + 1, :]
            at += 1
    copies = out_ref.shape[0] // table.shape[0]

    def deal(o, carry):
        row = table[pl.ds(owner_ref[o], 1), :]
        for c in range(copies):
            out_ref[pl.ds(o * copies + c, 1), :] = row
        return carry

    lax.fori_loop(0, table.shape[0], deal, 0)


def deal_lines(place, owner, lines, copies):
    smem = pl.BlockSpec(memory_space=pltpu.SMEM)
    vmem = pl.BlockSpec(memory_space=pltpu.VMEM)
    groups = owner.shape[0]
    return pl.pallas_call(
        table_kernel,
        out_shape=jax.ShapeDtypeStruct((groups * copies, LANES), jnp.float32),
        in_specs=[smem, smem] + [vmem] * len(lines),
        out_specs=vmem,
        scratch_shapes=[pltpu.VMEM((groups, LANES), jnp.float32)],
        compiler_params=pltpu.CompilerParams(vmem_limit_bytes=2 << 20),
        name="deal",
    )(place, owner, *lines)


def merge_kernel(length_ref, lines_ref, logprob_ref, entropy_ref):
    lines = lines_ref[...]
    total = pltpu.roll(lines, 96, 1)
    spread = pltpu.roll(lines, 64, 1)
    pick = pltpu.roll(lines, 32, 1)
    lane = lax.broadcasted_iota(jnp.int32, lines.shape, 1)
    live = (total > 0.0) & (lane < 32)
    peak = jnp.max(jnp.where(live, lines, -jnp.inf), axis=0, keepdims=True)
    scale = jnp.where(live, jnp.exp(lines - peak), 0.0)
    exp_total = jnp.sum(jnp.where(live, scale * total, 0.0), axis=0, keepdims=True)
    exp_spread = jnp.sum(jnp.where(live, scale * spread, 0.0), axis=0, keepdims=True)
    picked = jnp.sum(jnp.where(live, pick, 0.0), axis=0, keepdims=True)
    log_total = peak + jnp.log(exp_total)
    keep = lax.broadcasted_iota(jnp.int32, (1, LANES), 1) < length_ref[0]
    slots = logprob_ref.shape[0]
    logprob_ref[...] = jnp.where(keep, picked - log_total, 0.0)[0, :slots]
    entropy_ref[...] = jnp.where(keep, log_total - exp_spread / exp_total, 0.0)[0, :slots]


def merge(lengths, lines, slots):
    vmem = pl.BlockSpec(memory_space=pltpu.VMEM)
    shape = jax.ShapeDtypeStruct((slots,), jnp.float32)
    return pl.pallas_call(
        merge_kernel,
        out_shape=(shape, shape),
        in_specs=[pl.BlockSpec(memory_space=pltpu.SMEM), vmem],
        out_specs=(vmem, vmem),
        compiler_params=pltpu.CompilerParams(vmem_limit_bytes=4 << 20),
        name="merge",
    )(lengths, lines)


def places():
    zl, x, core = lax.axis_index("zl"), lax.axis_index("x"), lax.axis_index("core")
    outer, inner = jnp.where(core == 0, zl, x), jnp.where(core == 0, x, zl)

    def line(step, offset, halves):
        far, near = (outer + step) % 4, (inner + offset) % 4
        z, col = jnp.where(core == 0, far, near), jnp.where(core == 0, near, far)
        return [((half * 4 + z) * 4 + col) * 2 + core for half in halves]

    both = (0, 1)
    order = [(0, o) for o in (0, 3, 1, 2)] + [(3, 0), (3, 3), (1, 0), (1, 3)]
    order += [(3, 1), (3, 2), (1, 1), (1, 2), (2, 0), (2, 3), (2, 1), (2, 2)]
    return jnp.stack([w for step, offset in order for w in line(step, offset, both)]).astype(jnp.int32)


def local(hidden, gain, head_weight, token_ids, lengths, owner_device):
    core = lax.axis_index("core")
    cols, slots = head_weight.shape[1], hidden.shape[0]
    other_weight = lax.ppermute(head_weight, "core", [(0, 1), (1, 0)])
    chip = ((lax.axis_index("zh") * 4 + lax.axis_index("zl")) * 4 + lax.axis_index("x")) * 2
    base = lambda c: ((chip + c) * 4 + lax.axis_index("tp")) * cols
    bases = jnp.stack([base(core), base(1 - core)]).astype(jnp.int32)

    ids = token_ids[:, None]
    lane = lax.broadcasted_iota(jnp.int32, (slots, LANES), 1)
    digits = jnp.where(lane == 0, ids >> 12, jnp.where(lane == 1, (ids >> 6) & 63, jnp.where(lane == 2, ids & 63, 0)))
    block = jnp.concatenate([hidden, digits.astype(jnp.bfloat16)], axis=1)
    partner = lax.ppermute(block, "zh", [(0, 1), (1, 0)])
    around = lambda value: [value] + [lax.ppermute(value, "tp", [(i, (i - k) % 4) for i in range(4)]) for k in (1, 3, 2)]
    half, quarter = lax.axis_index("zh"), lax.axis_index("tp")
    spots = jnp.stack([half, 1 - half] + [(quarter + k) % 4 for k in (0, 1, 3, 2)]).astype(jnp.int32)
    own = norm(spots, around(block) + around(partner), gain)
    own, other_weight = lax.optimization_barrier((own, other_weight))

    both = (head_weight, other_weight)
    lines = ring(own, both, bases, slots)
    dealt = deal_lines(places(), owner_device, lines, 4)
    met = lax.all_to_all(dealt, ALL, 0, 0, tiled=True)
    return merge(lengths, met, slots)


def ring(own, both, bases, slots):
    def move(value, step, swap=False):
        return send(value, step, swap)

    def scored(parts):
        return score(parts, *both, bases)

    f1, b1 = move(own, 1, True), move(own, -1, True)
    first = jnp.concatenate([own, f1], axis=0)
    fa, ba = move(first, 1), move(first, -1)
    f2, b2 = move(f1[:slots], 1, True), move(b1[slots:], -1, True)
    second = jnp.concatenate([b1, f2, b2], axis=0)
    fb, bb = move(second, 1), move(second, -1)
    rows = slots * 2
    fc, bc = move(fa[:rows], 1), move(ba[rows:], -1)
    fd, bd = move(fb[:rows], 1), move(bb[rows:], -1)
    return [scored([first, second]), scored([fa, ba]), scored([fb, bb]), scored([fc, bc]), scored([fd, bd])]


def solution(mesh):
    split = Mesh(mesh.devices.reshape(SPLIT), ALL)
    placed = (P(REQ, "tp"), P(), P(None, ALL), P(REQ), P(REQ), P())
    return jax.shard_map(local, mesh=split, in_specs=placed, out_specs=(P(REQ), P(REQ)), check_vma=False)
```

profile of v0, /device:TPU:1, one launch (start us, length us, event | category | flops | bytes accessed | tf_op | source)
XLA Modules:
  0.0 143.4 jit_solution(9393640769684920248)
XLA Ops:
  0.6 3.3 %collective-permute-start.7 = (bf16[5120,512]{1,0:T(8,128)(2,1)}, bf16[5120,512]{1,0:T(8,128)(2,1)}, u32[]{:S(2)}, u32[]{:S(2)}) collective-permute-start(bf16[5120,512]{1,0:T(8,128)(2,1)} %refs_2_.9), channel_id=1, source_target_pairs={{0,4},{4,0},{1,5},{5,1},{2,6},{6,2},{3,7},{7,3},{8,12},{12,8},{9,1... | collective-permute-start | bytes 15728648 | tf_op jit(solution)/shard_map/ppermute | solution.py:210
  3.9 0.7 broadcast_shift-right-arithmetic_fusion
  4.6 0.1 select_convert_fusion
  4.7 0.9 pad_maximum_fusion.refs_0_
  5.6 5.2 %collective-permute-start.3 = (bf16[32,1408]{1,0:T(8,128)(2,1)S(1)}, bf16[32,1408]{1,0:T(8,128)(2,1)S(1)}, u32[]{:S(2)}, u32[]{:S(2)}) collective-permute-start(bf16[32,1408]{1,0:T(8,128)(2,1)S(1)} %pad_maximum_fusion.refs_0_), channel_id=1, source_target_pairs={{0,128},{128,0},{1,129},{129,1},{2,130},{130,2},{3,131},{131,3},{4... | collective-permute-start | bytes 270344 | tf_op jit(solution)/shard_map/ppermute | solution.py:219
  10.8 2.9 %collective-permute-start.2 = (bf16[32,1408]{1,0:T(8,128)(2,1)S(1)}, bf16[32,1408]{1,0:T(8,128)(2,1)S(1)}, u32[]{:S(2)}, u32[]{:S(2)}) collective-permute-start(bf16[32,1408]{1,0:T(8,128)(2,1)S(1)} %pad_maximum_fusion.refs_0_), channel_id=1, source_target_pairs={{0,2},{1,3},{2,0},{3,1},{4,6},{5,7},{6,4},{7,5},{8,10},{9,11},{10,... | collective-permute-start | bytes 270344 | tf_op jit(solution)/shard_map/ppermute | solution.py:220
  13.7 0.4 collective-permute-start.1
  14.1 2.3 %collective-permute-start = (bf16[32,1408]{1,0:T(8,128)(2,1)S(1)}, bf16[32,1408]{1,0:T(8,128)(2,1)S(1)}, u32[]{:S(2)}, u32[]{:S(2)}) collective-permute-start(bf16[32,1408]{1,0:T(8,128)(2,1)S(1)} %pad_maximum_fusion.refs_0_), channel_id=1, source_target_pairs={{0,3},{1,0},{2,1},{3,2},{4,7},{5,4},{6,5},{7,6},{8,11},{9,8},{10,9... | collective-permute-start | bytes 270344 | tf_op jit(solution)/shard_map/ppermute | solution.py:220
  16.4 0.0 collective-permute-done.3.refs_4_
  16.4 0.3 collective-permute-start.6
  16.6 0.0 collective-permute-done.2.refs_3_
  16.7 0.8 collective-permute-start.5
  17.4 0.8 collective-permute-done.1.refs_2_
  18.3 1.1 collective-permute-start.4
  19.3 0.1 stack.171.spot_ref
  19.4 0.0 collective-permute-done.refs_1_
  19.4 1.9 %collective-permute-done.6.refs_7_ = bf16[32,1408]{1,0:T(8,128)(2,1)S(1)} collective-permute-done((bf16[32,1408]{1,0:T(8,128)(2,1)S(1)}, bf16[32,1408]{1,0:T(8,128)(2,1)S(1)}, u32[]{:S(2)}, u32[]{:S(2)}) %collective-permute-start.6) | collective-permute-done | bytes 90144 | tf_op jit(solution)/shard_map/ppermute | solution.py:220
  21.4 2.6 %collective-permute-done.5.refs_6_ = bf16[32,1408]{1,0:T(8,128)(2,1)S(1)} collective-permute-done((bf16[32,1408]{1,0:T(8,128)(2,1)S(1)}, bf16[32,1408]{1,0:T(8,128)(2,1)S(1)}, u32[]{:S(2)}, u32[]{:S(2)}) %collective-permute-start.5) | collective-permute-done | bytes 90144 | tf_op jit(solution)/shard_map/ppermute | solution.py:220
  23.9 0.0 collective-permute-done.4.refs_5_
  24.0 0.7 copy-done.1
  24.7 0.9 norm.1
  25.6 0.0 collective-permute-done.7.refs_3_
  25.6 2.3 %collective-permute-start.9 = (bf16[64,5248]{1,0:T(8,128)(2,1)S(1)}, bf16[64,5248]{1,0:T(8,128)(2,1)S(1)}, u32[]{:S(2)}, u32[]{:S(2)}) collective-permute-start(bf16[64,5248]{1,0:T(8,128)(2,1)S(1)} %norm.1), channel_id=1, source_target_pairs={{0,24},{4,228},{8,0},{12,236},{16,8},{20,244},{24,16},{28,252},{32... | collective-permute-start | bytes 2015240 | tf_op jit(solution)/shard_map/ppermute | solution.py:31
  27.9 0.0 collective-permute-start.8
  27.9 1.0 constant_dynamic-update-slice_fusion.1
  28.8 10.2 %collective-permute-done.8 = bf16[64,5248]{1,0:T(8,128)(2,1)S(1)} collective-permute-done((bf16[64,5248]{1,0:T(8,128)(2,1)S(1)}, bf16[64,5248]{1,0:T(8,128)(2,1)S(1)}, u32[]{:S(2)}, u32[]{:S(2)}) %collective-permute-start.8) | collective-permute-done | bytes 671776 | tf_op jit(solution)/shard_map/ppermute | solution.py:31
  39.0 0.9 constant_dynamic-update-slice_fusion.refs_0_
  39.9 2.2 %collective-permute-start.13 = (bf16[128,5248]{1,0:T(8,128)(2,1)}, bf16[128,5248]{1,0:T(8,128)(2,1)S(1)}, u32[]{:S(2)}, u32[]{:S(2)}) collective-permute-start(bf16[128,5248]{1,0:T(8,128)(2,1)} %constant_dynamic-update-slice_fusion.refs_0_), channel_id=1, source_target_pairs={{0,224},{4,28},{8,232},{12,4},{16,240},{20,12},{24,248},{28,20},{3... | collective-permute-start | bytes 4030472 | tf_op jit(solution)/shard_map/ppermute | solution.py:31
  42.1 0.0 collective-permute-start.12
  42.1 0.0 collective-permute-done.9
  42.2 0.6 collective-permute-start.11
  42.8 1.0 collective-permute-start.10
  43.8 0.9 constant_dynamic-update-slice_fusion.4
  44.7 5.4 %collective-permute-done.10 = bf16[32,5248]{1,0:T(8,128)(2,1)S(1)} collective-permute-done((bf16[32,5248]{1,0:T(8,128)(2,1)S(1)}, bf16[32,5248]{1,0:T(8,128)(2,1)S(1)}, u32[]{:S(2)}, u32[]{:S(2)}) %collective-permute-start.10) | collective-permute-done | bytes 335904 | tf_op jit(solution)/shard_map/ppermute | solution.py:31
  50.1 0.8 constant_dynamic-update-slice_fusion.3
  50.9 0.7 collective-permute-done.11
  51.5 0.8 constant_dynamic-update-slice_fusion.2.refs_1_
  52.3 5.6 %collective-permute-start.15 = (bf16[128,5248]{1,0:T(8,128)(2,1)}, bf16[128,5248]{1,0:T(8,128)(2,1)}, u32[]{:S(2)}, u32[]{:S(2)}) collective-permute-start(bf16[128,5248]{1,0:T(8,128)(2,1)} %constant_dynamic-update-slice_fusion.2.refs_1_), channel_id=1, source_target_pairs={{0,224},{4,28},{8,232},{12,4},{16,240},{20,12},{24,248},{28,20},{3... | collective-permute-start | bytes 4030472 | tf_op jit(solution)/shard_map/ppermute | solution.py:31
  57.9 0.0 collective-permute-start.14
  57.9 0.1 stack.161.place_ref
  58.0 0.1 pad_add_fusion.base_ref
  58.1 2.8 %collective-permute-done.13.refs_1_ = bf16[128,5248]{1,0:T(8,128)(2,1)S(1)} collective-permute-done((bf16[128,5248]{1,0:T(8,128)(2,1)}, bf16[128,5248]{1,0:T(8,128)(2,1)S(1)}, u32[]{:S(2)}, u32[]{:S(2)}) %collective-permute-start.13) | collective-permute-done | bytes 1343520 | tf_op jit(solution)/shard_map/ppermute | solution.py:31
  61.0 3.4 %collective-permute-start.17 = (bf16[64,5248]{1,0:T(8,128)(2,1)S(1)}, bf16[64,5248]{1,0:T(8,128)(2,1)S(1)}, u32[]{:S(2)}, u32[]{:S(2)}) collective-permute-start(bf16[64,5248]{1,0:T(8,128)(2,1)S(1)} %slice.27), channel_id=1, source_target_pairs={{0,224},{4,28},{8,232},{12,4},{16,240},{20,12},{24,248},{28,20},{3... | collective-permute-start | bytes 2015240 | tf_op jit(solution)/shard_map/ppermute | solution.py:31
  64.4 0.0 collective-permute-done.12.refs_0_
  64.4 0.1 collective-permute-start.16
  64.5 10.8 %collective-permute-done.15.refs_1_ = bf16[128,5248]{1,0:T(8,128)(2,1)} collective-permute-done((bf16[128,5248]{1,0:T(8,128)(2,1)}, bf16[128,5248]{1,0:T(8,128)(2,1)}, u32[]{:S(2)}, u32[]{:S(2)}) %collective-permute-start.15) | collective-permute-done | bytes 1343520 | tf_op jit(solution)/shard_map/ppermute | solution.py:31
  75.4 1.1 slice.29
  76.5 3.5 %collective-permute-start.19 = (bf16[64,5248]{1,0:T(8,128)(2,1)S(1)}, bf16[64,5248]{1,0:T(8,128)(2,1)S(1)}, u32[]{:S(2)}, u32[]{:S(2)}) collective-permute-start(bf16[64,5248]{1,0:T(8,128)(2,1)S(1)} %slice.29), channel_id=1, source_target_pairs={{0,224},{4,28},{8,232},{12,4},{16,240},{20,12},{24,248},{28,20},{3... | collective-permute-start | bytes 2015240 | tf_op jit(solution)/shard_map/ppermute | solution.py:31
  80.0 0.0 collective-permute-done.14.refs_0_
  80.0 1.1 slice.28
  81.1 0.1 collective-permute-start.18
  81.2 8.4 %score.5.refs_0_ = f32[8,128]{1,0:T(8,128)S(1)} custom-call(s32[2]{0:T(128)S(1)} %pad_add_fusion.base_ref, bf16[128,5248]{1,0:T(8,128)(2,1)} %constant_dynamic-update-slice_fusion.refs_0_, bf16[128,5248]{1,0:T(8,128)(2,1)} %constant_dynamic-update-slice_fusion.2.refs_1_, bf16[5120,512]{1,0:T(8,128)(2,1)S(1)} %copy-done, ...), custom_call_target="tpu_custom_call" | custom-call | flops 2684354560 | bytes 2621440 | tf_op jit(solution)/shard_map/score/pallas_call | solution.py:112
  89.6 7.6 %score.6.refs_1_ = f32[8,128]{1,0:T(8,128)S(1)} custom-call(s32[2]{0:T(128)S(1)} %pad_add_fusion.base_ref, bf16[128,5248]{1,0:T(8,128)(2,1)S(1)} %collective-permute-done.12.refs_0_, bf16[128,5248]{1,0:T(8,128)(2,1)S(1)} %collective-permute-done.13.refs_1_, bf16[5120,512]{1,0:T(8,128)(2,1)S(1)} %copy-done, bf16[5120,512]{1,0:T(8,128)(2,1)} %collective-permute-done.7.refs_3_), custom_call_target="tpu_custom_call" | custom-call | flops 2684354560 | bytes 2621440 | tf_op jit(solution)/shard_map/score/pallas_call | solution.py:112
  97.2 8.4 %score.7.refs_2_ = f32[8,128]{1,0:T(8,128)S(1)} custom-call(s32[2]{0:T(128)S(1)} %pad_add_fusion.base_ref, bf16[128,5248]{1,0:T(8,128)(2,1)} %collective-permute-done.14.refs_0_, bf16[128,5248]{1,0:T(8,128)(2,1)} %collective-permute-done.15.refs_1_, bf16[5120,512]{1,0:T(8,128)(2,1)S(1)} %copy-done, bf16[5120,512]{1,0:T(8,128)(2,1)} %collective-permute-done.7.refs_3_), custom_call_target="tpu_custom_call" | custom-call | flops 2684354560 | bytes 2621440 | tf_op jit(solution)/shard_map/score/pallas_call | solution.py:112
  105.6 0.0 collective-permute-done.17.refs_1_
  105.6 0.0 collective-permute-done.16.refs_0_
  105.6 5.5 %score.8.refs_3_ = f32[4,128]{1,0:T(4,128)S(1)} custom-call(s32[2]{0:T(128)S(1)} %pad_add_fusion.base_ref, bf16[64,5248]{1,0:T(8,128)(2,1)S(1)} %collective-permute-done.16.refs_0_, bf16[64,5248]{1,0:T(8,128)(2,1)S(1)} %collective-permute-done.17.refs_1_, bf16[5120,512]{1,0:T(8,128)(2,1)S(1)} %copy-done, bf16[5120,512]{1,0:T(8,128)(2,1)} %collective-permute-done.7.refs_3_), custom_call_target="tpu_custom_call" | custom-call | flops 1342177280 | bytes 1310720 | tf_op jit(solution)/shard_map/score/pallas_call | solution.py:112
  111.1 0.0 copy-start.2
  111.2 0.0 collective-permute-done.18.refs_0_
  111.2 5.5 %score.9.refs_4_ = f32[4,128]{1,0:T(4,128)S(1)} custom-call(s32[2]{0:T(128)S(1)} %pad_add_fusion.base_ref, bf16[64,5248]{1,0:T(8,128)(2,1)S(1)} %collective-permute-done.18.refs_0_, bf16[64,5248]{1,0:T(8,128)(2,1)S(1)} %collective-permute-done.19.refs_1_, bf16[5120,512]{1,0:T(8,128)(2,1)S(1)} %copy-done, bf16[5120,512]{1,0:T(8,128)(2,1)} %collective-permute-done.7.refs_3_), custom_call_target="tpu_custom_call" | custom-call | flops 1342177280 | bytes 1310720 | tf_op jit(solution)/shard_map/score/pallas_call | solution.py:112
  116.7 1.6 %deal.1 = f32[256,128]{1,0:T(8,128)} custom-call(s32[32]{0:T(128)S(1)} %stack.161.place_ref, s32[64]{0:T(128)S(1)} %copy-done.2, f32[8,128]{1,0:T(8,128)S(1)} %score.5.refs_0_, f32[8,128]{1,0:T(8,128)S(1)} %score.6.refs_1_, f32[8,128]{1,0:T(8,128)S(1)} %score.7.refs_2_, f32[4,128]{1,0:T(4,128)S(1)} %score.8.refs_3_, f32[4,128]{1,0:T(4,128)S(1)} %score.9.refs_4_), custom_call_target="tpu_custom_call" | custom-call | tf_op jit(solution)/shard_map/deal/pallas_call | solution.py:149
  118.3 11.6 %all-to-all-start = ((f32[256,1,128]{2,1,0:T(1,128)}), f32[256,1,128]{2,1,0:T(1,128)S(1)}, u32[]{:S(2)}, u32[]{:S(2)}) async-start(f32[256,1,128]{2,1,0:T(1,128)} %bitcast.42), calls=%async_computation | async-start | bytes 262144 | tf_op jit(solution)/shard_map/all_to_all | solution.py:229
  130.6 12.1 %all-to-all-done = f32[256,1,128]{2,1,0:T(1,128)S(1)} async-done(((f32[256,1,128]{2,1,0:T(1,128)}), f32[256,1,128]{2,1,0:T(1,128)S(1)}, u32[]{:S(2)}, u32[]{:S(2)}) %all-to-all-start) | async-done | bytes 131104 | tf_op jit(solution)/shard_map/all_to_all | solution.py:229
  142.7 0.7 merge.1
  (11 shorter events, 0.2 us)
Async XLA Ops:
  0.6 24.9 %collective-permute-start.7 = (bf16[5120,512]{1,0:T(8,128)(2,1)}, bf16[5120,512]{1,0:T(8,128)(2,1)}, u32[]{:S(2)}, u32[]{:S(2)}) collective-permute-start(bf16[5120,512]{1,0:T(8,128)(2,1)} %refs_2_.9), channel_id=1, source_target_pairs={{0,4},{4,0},{1,5},{5,1},{2,6},{6,2},{3,7},{7,3},{8,12},{12,8},{9,1... | collective-permute-start | bytes 15728648 | tf_op jit(solution)/shard_map/ppermute | solution.py:210
  5.6 10.8 %collective-permute-start.3 = (bf16[32,1408]{1,0:T(8,128)(2,1)S(1)}, bf16[32,1408]{1,0:T(8,128)(2,1)S(1)}, u32[]{:S(2)}, u32[]{:S(2)}) collective-permute-start(bf16[32,1408]{1,0:T(8,128)(2,1)S(1)} %pad_maximum_fusion.refs_0_), channel_id=1, source_target_pairs={{0,128},{128,0},{1,129},{129,1},{2,130},{130,2},{3,131},{131,3},{4... | collective-permute-start | bytes 270344 | tf_op jit(solution)/shard_map/ppermute | solution.py:219
  10.8 5.9 %collective-permute-start.2 = (bf16[32,1408]{1,0:T(8,128)(2,1)S(1)}, bf16[32,1408]{1,0:T(8,128)(2,1)S(1)}, u32[]{:S(2)}, u32[]{:S(2)}) collective-permute-start(bf16[32,1408]{1,0:T(8,128)(2,1)S(1)} %pad_maximum_fusion.refs_0_), channel_id=1, source_target_pairs={{0,2},{1,3},{2,0},{3,1},{4,6},{5,7},{6,4},{7,5},{8,10},{9,11},{10,... | collective-permute-start | bytes 270344 | tf_op jit(solution)/shard_map/ppermute | solution.py:220
  13.7 4.6 %collective-permute-start.1 = (bf16[32,1408]{1,0:T(8,128)(2,1)S(1)}, bf16[32,1408]{1,0:T(8,128)(2,1)S(1)}, u32[]{:S(2)}, u32[]{:S(2)}) collective-permute-start(bf16[32,1408]{1,0:T(8,128)(2,1)S(1)} %pad_maximum_fusion.refs_0_), channel_id=1, source_target_pairs={{0,1},{1,2},{2,3},{3,0},{4,5},{5,6},{6,7},{7,4},{8,9},{9,10},{10,1... | collective-permute-start | bytes 270344 | tf_op jit(solution)/shard_map/ppermute | solution.py:220
  14.1 5.3 %collective-permute-start = (bf16[32,1408]{1,0:T(8,128)(2,1)S(1)}, bf16[32,1408]{1,0:T(8,128)(2,1)S(1)}, u32[]{:S(2)}, u32[]{:S(2)}) collective-permute-start(bf16[32,1408]{1,0:T(8,128)(2,1)S(1)} %pad_maximum_fusion.refs_0_), channel_id=1, source_target_pairs={{0,3},{1,0},{2,1},{3,2},{4,7},{5,4},{6,5},{7,6},{8,11},{9,8},{10,9... | collective-permute-start | bytes 270344 | tf_op jit(solution)/shard_map/ppermute | solution.py:220
  16.4 5.0 %collective-permute-start.6 = (bf16[32,1408]{1,0:T(8,128)(2,1)S(1)}, bf16[32,1408]{1,0:T(8,128)(2,1)S(1)}, u32[]{:S(2)}, u32[]{:S(2)}) collective-permute-start(bf16[32,1408]{1,0:T(8,128)(2,1)S(1)} %collective-permute-done.3.refs_4_), channel_id=1, source_target_pairs={{0,2},{1,3},{2,0},{3,1},{4,6},{5,7},{6,4},{7,5},{8,10},{9,11},{10,... | collective-permute-start | bytes 270344 | tf_op jit(solution)/shard_map/ppermute | solution.py:220
  16.7 7.3 %collective-permute-start.5 = (bf16[32,1408]{1,0:T(8,128)(2,1)S(1)}, bf16[32,1408]{1,0:T(8,128)(2,1)S(1)}, u32[]{:S(2)}, u32[]{:S(2)}) collective-permute-start(bf16[32,1408]{1,0:T(8,128)(2,1)S(1)} %collective-permute-done.3.refs_4_), channel_id=1, source_target_pairs={{0,1},{1,2},{2,3},{3,0},{4,5},{5,6},{6,7},{7,4},{8,9},{9,10},{10,1... | collective-permute-start | bytes 270344 | tf_op jit(solution)/shard_map/ppermute | solution.py:220
  18.3 5.7 %collective-permute-start.4 = (bf16[32,1408]{1,0:T(8,128)(2,1)S(1)}, bf16[32,1408]{1,0:T(8,128)(2,1)S(1)}, u32[]{:S(2)}, u32[]{:S(2)}) collective-permute-start(bf16[32,1408]{1,0:T(8,128)(2,1)S(1)} %collective-permute-done.3.refs_4_), channel_id=1, source_target_pairs={{0,3},{1,0},{2,1},{3,2},{4,7},{5,4},{6,5},{7,6},{8,11},{9,8},{10,9... | collective-permute-start | bytes 270344 | tf_op jit(solution)/shard_map/ppermute | solution.py:220
  23.9 0.7 copy-start.1
  25.6 16.6 %collective-permute-start.9 = (bf16[64,5248]{1,0:T(8,128)(2,1)S(1)}, bf16[64,5248]{1,0:T(8,128)(2,1)S(1)}, u32[]{:S(2)}, u32[]{:S(2)}) collective-permute-start(bf16[64,5248]{1,0:T(8,128)(2,1)S(1)} %norm.1), channel_id=1, source_target_pairs={{0,24},{4,228},{8,0},{12,236},{16,8},{20,244},{24,16},{28,252},{32... | collective-permute-start | bytes 2015240 | tf_op jit(solution)/shard_map/ppermute | solution.py:31
  27.9 11.1 %collective-permute-start.8 = (bf16[64,5248]{1,0:T(8,128)(2,1)S(1)}, bf16[64,5248]{1,0:T(8,128)(2,1)S(1)}, u32[]{:S(2)}, u32[]{:S(2)}) collective-permute-start(bf16[64,5248]{1,0:T(8,128)(2,1)S(1)} %norm.1), channel_id=1, source_target_pairs={{0,8},{4,36},{8,16},{12,44},{16,24},{20,52},{24,0},{28,60},{32,40}... | collective-permute-start | bytes 2015240 | tf_op jit(solution)/shard_map/ppermute | solution.py:31
  39.9 21.0 %collective-permute-start.13 = (bf16[128,5248]{1,0:T(8,128)(2,1)}, bf16[128,5248]{1,0:T(8,128)(2,1)S(1)}, u32[]{:S(2)}, u32[]{:S(2)}) collective-permute-start(bf16[128,5248]{1,0:T(8,128)(2,1)} %constant_dynamic-update-slice_fusion.refs_0_), channel_id=1, source_target_pairs={{0,224},{4,28},{8,232},{12,4},{16,240},{20,12},{24,248},{28,20},{3... | collective-permute-start | bytes 4030472 | tf_op jit(solution)/shard_map/ppermute | solution.py:31
  42.1 22.3 %collective-permute-start.12 = (bf16[128,5248]{1,0:T(8,128)(2,1)}, bf16[128,5248]{1,0:T(8,128)(2,1)S(1)}, u32[]{:S(2)}, u32[]{:S(2)}) collective-permute-start(bf16[128,5248]{1,0:T(8,128)(2,1)} %constant_dynamic-update-slice_fusion.refs_0_), channel_id=1, source_target_pairs={{0,32},{4,12},{8,40},{12,20},{16,48},{20,28},{24,56},{28,4},{32,64... | collective-permute-start | bytes 4030472 | tf_op jit(solution)/shard_map/ppermute | solution.py:31
  42.2 9.4 %collective-permute-start.11 = (bf16[32,5248]{1,0:T(8,128)(2,1)S(1)}, bf16[32,5248]{1,0:T(8,128)(2,1)S(1)}, u32[]{:S(2)}, u32[]{:S(2)}) collective-permute-start(bf16[32,5248]{1,0:T(8,128)(2,1)S(1)} %slice.25), channel_id=1, source_target_pairs={{0,24},{4,228},{8,0},{12,236},{16,8},{20,244},{24,16},{28,252},{32... | collective-permute-start | bytes 1007624 | tf_op jit(solution)/shard_map/ppermute | solution.py:31
  42.8 7.3 %collective-permute-start.10 = (bf16[32,5248]{1,0:T(8,128)(2,1)S(1)}, bf16[32,5248]{1,0:T(8,128)(2,1)S(1)}, u32[]{:S(2)}, u32[]{:S(2)}) collective-permute-start(bf16[32,5248]{1,0:T(8,128)(2,1)S(1)} %slice.24), channel_id=1, source_target_pairs={{0,8},{4,36},{8,16},{12,44},{16,24},{20,52},{24,0},{28,60},{32,40}... | collective-permute-start | bytes 1007624 | tf_op jit(solution)/shard_map/ppermute | solution.py:31
  52.3 23.1 %collective-permute-start.15 = (bf16[128,5248]{1,0:T(8,128)(2,1)}, bf16[128,5248]{1,0:T(8,128)(2,1)}, u32[]{:S(2)}, u32[]{:S(2)}) collective-permute-start(bf16[128,5248]{1,0:T(8,128)(2,1)} %constant_dynamic-update-slice_fusion.2.refs_1_), channel_id=1, source_target_pairs={{0,224},{4,28},{8,232},{12,4},{16,240},{20,12},{24,248},{28,20},{3... | collective-permute-start | bytes 4030472 | tf_op jit(solution)/shard_map/ppermute | solution.py:31
  57.9 22.0 %collective-permute-start.14 = (bf16[128,5248]{1,0:T(8,128)(2,1)}, bf16[128,5248]{1,0:T(8,128)(2,1)}, u32[]{:S(2)}, u32[]{:S(2)}) collective-permute-start(bf16[128,5248]{1,0:T(8,128)(2,1)} %constant_dynamic-update-slice_fusion.2.refs_1_), channel_id=1, source_target_pairs={{0,32},{4,12},{8,40},{12,20},{16,48},{20,28},{24,56},{28,4},{32,64... | collective-permute-start | bytes 4030472 | tf_op jit(solution)/shard_map/ppermute | solution.py:31
  60.9 20.3 %copy-start = (bf16[5120,512]{1,0:T(8,128)(2,1)S(1)}, bf16[5120,512]{1,0:T(8,128)(2,1)}, u32[]{:S(2)}) copy-start(bf16[5120,512]{1,0:T(8,128)(2,1)} %refs_2_.9) | copy-start | bytes 15728644
  61.0 44.6 %collective-permute-start.17 = (bf16[64,5248]{1,0:T(8,128)(2,1)S(1)}, bf16[64,5248]{1,0:T(8,128)(2,1)S(1)}, u32[]{:S(2)}, u32[]{:S(2)}) collective-permute-start(bf16[64,5248]{1,0:T(8,128)(2,1)S(1)} %slice.27), channel_id=1, source_target_pairs={{0,224},{4,28},{8,232},{12,4},{16,240},{20,12},{24,248},{28,20},{3... | collective-permute-start | bytes 2015240 | tf_op jit(solution)/shard_map/ppermute | solution.py:31
  64.4 41.2 %collective-permute-start.16 = (bf16[64,5248]{1,0:T(8,128)(2,1)S(1)}, bf16[64,5248]{1,0:T(8,128)(2,1)S(1)}, u32[]{:S(2)}, u32[]{:S(2)}) collective-permute-start(bf16[64,5248]{1,0:T(8,128)(2,1)S(1)} %slice.26), channel_id=1, source_target_pairs={{0,32},{4,12},{8,40},{12,20},{16,48},{20,28},{24,56},{28,4},{32,64... | collective-permute-start | bytes 2015240 | tf_op jit(solution)/shard_map/ppermute | solution.py:31
  76.5 34.7 %collective-permute-start.19 = (bf16[64,5248]{1,0:T(8,128)(2,1)S(1)}, bf16[64,5248]{1,0:T(8,128)(2,1)S(1)}, u32[]{:S(2)}, u32[]{:S(2)}) collective-permute-start(bf16[64,5248]{1,0:T(8,128)(2,1)S(1)} %slice.29), channel_id=1, source_target_pairs={{0,224},{4,28},{8,232},{12,4},{16,240},{20,12},{24,248},{28,20},{3... | collective-permute-start | bytes 2015240 | tf_op jit(solution)/shard_map/ppermute | solution.py:31
  81.1 30.1 %collective-permute-start.18 = (bf16[64,5248]{1,0:T(8,128)(2,1)S(1)}, bf16[64,5248]{1,0:T(8,128)(2,1)S(1)}, u32[]{:S(2)}, u32[]{:S(2)}) collective-permute-start(bf16[64,5248]{1,0:T(8,128)(2,1)S(1)} %slice.28), channel_id=1, source_target_pairs={{0,32},{4,12},{8,40},{12,20},{16,48},{20,28},{24,56},{28,4},{32,64... | collective-permute-start | bytes 2015240 | tf_op jit(solution)/shard_map/ppermute | solution.py:31
  111.1 5.6 %copy-start.2 = (s32[64]{0:T(128)S(1)}, s32[64]{0:T(128)}, u32[]{:S(2)}) copy-start(s32[64]{0:T(128)} %owner_ref.1) | copy-start | bytes 772
  118.3 24.3 %all-to-all-start = ((f32[256,1,128]{2,1,0:T(1,128)}), f32[256,1,128]{2,1,0:T(1,128)S(1)}, u32[]{:S(2)}, u32[]{:S(2)}) async-start(f32[256,1,128]{2,1,0:T(1,128)} %bitcast.42), calls=%async_computation | async-start | bytes 262144 | tf_op jit(solution)/shard_map/all_to_all | solution.py:229
where the time goes:
time: 144 us; the launch traced here: 143 us
  waiting for transfers between devices  47.3 us (33%)
  starting transfers between devices  46.6 us (32%)
  Pallas kernels  38.6 us (27%)
  local copies, waits for them, and re-layouts  7.66 us (5%)
  other arithmetic  1.73 us (1%)
  between operations  1.45 us (1%)
    pallas_call x5, Pallas kernels, score(): pl.pallas_call(functools.partial(score_kernel, n, width), out_shape=jax.S...  35.4 us
    ppermute x12, waiting for transfers between devices, send(): return lax.ppermute(value, REQ, pairs(step, swap))  29.9 us
    ppermute x12, starting transfers between devices, send(): return lax.ppermute(value, REQ, pairs(step, swap))  18.8 us
    all_to_all x1, waiting for transfers between devices, local(): met = lax.all_to_all(dealt, ALL, 0, 0, tiled=True)  12.1 us
    all_to_all x1, starting transfers between devices, local(): met = lax.all_to_all(dealt, ALL, 0, 0, tiled=True)  11.6 us
    ppermute x6, starting transfers between devices, local(): lax.ppermute(value, 'tp', [(i, (i - k) % 4) for i in range(4)])  7.72 us
    ppermute x6, waiting for transfers between devices, local(): lax.ppermute(value, 'tp', [(i, (i - k) % 4) for i in range(4)])  5.37 us
    ppermute x1, starting transfers between devices, local(): partner = lax.ppermute(block, 'zh', [(0, 1), (1, 0)])  5.2 us
  transfers between devices with their start and end apart: 21, of which 9 were waited for; matrix products, arithmetic and copies ran while one was open for 6% of the time, Pallas kernels for 21%

commit v1 on v0

--- a/solution.py
+++ b/solution.py
@@ -2,6 +2,7 @@
 
 import jax
 import jax.numpy as jnp
+import numpy as np
 from jax import lax
 from jax.experimental import pallas as pl
 from jax.experimental.pallas import tpu as pltpu
@@ -37,14 +38,14 @@
     rows = pieces[0].shape[0]
     for h in range(2):
         mine = pieces[h * quarters : (h + 1) * quarters]
-        at = pl.ds(pl.multiple_of(spot_ref[h] * rows, rows), rows)
+        at = pl.ds(pl.multiple_of(spot_ref[PLACES + h] * rows, rows), rows)
         square = jnp.zeros((rows, 1), jnp.float32)
         for piece in mine:
             values = piece[:, :width].astype(jnp.float32)
             square += jnp.sum(values * values, axis=1, keepdims=True)
         scale = lax.rsqrt(square / (width * quarters) + eps)
         for q, piece in enumerate(mine):
-            columns = pl.ds(pl.multiple_of(spot_ref[2 + q] * width, LANES), width)
+            columns = pl.ds(pl.multiple_of(spot_ref[PLACES + 2 + q] * width, LANES), width)
             values = piece[:, :width].astype(jnp.float32)
             out_ref[at, columns] = (values * scale * gain_ref[:, columns]).astype(jnp.bfloat16)
         out_ref[at, quarters * width :] = mine[0][:, width:]
@@ -62,32 +63,45 @@
     )(spots, *pieces, gain[None, :])
 
 
-def score_kernel(n_parts, width, base_ref, *refs):
-    parts, (w_own, w_other, out_ref, logits) = refs[:n_parts], refs[n_parts:]
-    rows = parts[0].shape[0]
+TILE = 256
+
+
+def score_kernel(sizes, width, base_ref, *refs):
+    n = len(sizes)
+    parts, (w_own, w_other, out_ref, logits, weights, sems) = refs[:n], refs[n:]
     cols = w_own.shape[1]
-    tile = 256
-    for half, w in enumerate((w_own, w_other)):
-
-        def column_tile(n, carry, half=half, w=w):
-            at = pl.multiple_of(n * tile, tile)
-            lhs = jnp.concatenate([part[:, :width] for part in parts], axis=0)
-            product = jnp.dot(lhs, w[:, pl.ds(at, tile)], preferred_element_type=jnp.float32)
-            logits[:, pl.ds(pl.multiple_of(half * cols + n * tile, tile), tile)] = product
-            return carry
-
-        lax.fori_loop(0, cols // tile, column_tile, 0)
+    per_half = cols // TILE
+
+    def fetch(half, n):
+        source = (w_own, w_other)[half].at[:, pl.ds(n * TILE, TILE)]
+        slot = half * per_half + n
+        return pltpu.make_async_copy(source, weights.at[slot], sems.at[slot])
+
+    for half in range(2):
+        for i in range(per_half):
+            fetch(half, i).start()
+
+    def column_tile(slot, carry):
+        pltpu.make_async_copy(w_own.at[:, pl.ds(0, TILE)], weights.at[slot], sems.at[slot]).wait()
+        lhs = jnp.concatenate([part[:, :width] for part in parts], axis=0)
+        product = jnp.dot(lhs, weights[slot], preferred_element_type=jnp.float32)
+        logits[:, pl.ds(pl.multiple_of(slot * TILE, TILE), TILE)] = product
+        return carry
+
+    lax.fori_loop(0, 2 * per_half, column_tile, 0)
 
     lane = lax.broadcasted_iota(jnp.int32, (32, LANES), 1)
     slot = lax.broadcasted_iota(jnp.int32, (32, LANES), 0)
     column = lax.broadcasted_iota(jnp.int32, (32, 2 * cols), 1)
-    vocab = jnp.where(column < cols, base_ref[0] + column, base_ref[1] + column - cols)
+    first_base, second_base = (base_ref[PLACES + SPOTS + i] * cols for i in range(2))
+    vocab = jnp.where(column < cols, first_base + column, second_base + column - cols)
     digit = jnp.where(lane == 0, 4096.0, jnp.where(lane == 1, 64.0, jnp.where(lane == 2, 1.0, 0.0)))
-    for i, part in enumerate(parts):
-
-        def group(g, carry, i=i, part=part):
+    before = 0
+    for part, rows in zip(parts, sizes):
+
+        def group(g, carry, part=part, before=before):
             row = pl.multiple_of(g * 32, 32)
-            lg = logits[pl.ds(pl.multiple_of(i * rows + g * 32, 32), 32), :]
+            lg = logits[pl.ds(pl.multiple_of(before + g * 32, 32), 32), :]
             code = part[pl.ds(row, 32), pl.ds(width, LANES)].astype(jnp.float32)
             ids = jnp.sum(code * digit, axis=1, keepdims=True).astype(jnp.int32)
             peak = jnp.max(lg, axis=1, keepdims=True)
@@ -97,28 +111,33 @@
             pick = jnp.sum(jnp.where(vocab == ids, lg, 0.0), axis=1, keepdims=True)
             stat = jnp.where(lane < 32, peak, jnp.where(lane < 64, total, jnp.where(lane < 96, spread, pick)))
             line = jnp.sum(jnp.where(lane % 32 == slot, stat, 0.0), axis=0, keepdims=True)
-            out_ref[pl.ds(i * (rows // 32) + g, 1), :] = line
+            out_ref[pl.ds(before // 32 + g, 1), :] = line
             return carry
 
         lax.fori_loop(0, rows // 32, group, 0)
+        before += rows
 
 
 def score(parts, w_own, w_other, bases):
-    rows = parts[0].shape[0]
-    n = len(parts)
-    width = w_own.shape[0]
-    cols = w_own.shape[1]
-    vmem = pl.BlockSpec(memory_space=pltpu.VMEM)
-    return pl.pallas_call(
-        functools.partial(score_kernel, n, width),
-        out_shape=jax.ShapeDtypeStruct((n * rows // 32, LANES), jnp.float32),
-        in_specs=[pl.BlockSpec(memory_space=pltpu.SMEM)] + [vmem] * (n + 2),
+    sizes = tuple(part.shape[0] for part in parts)
+    rows = sum(sizes)
+    width, cols = w_own.shape
+    vmem = pl.BlockSpec(memory_space=pltpu.VMEM)
+    hbm = pl.BlockSpec(memory_space=pltpu.HBM)
+    return pl.pallas_call(
+        functools.partial(score_kernel, sizes, width),
+        out_shape=jax.ShapeDtypeStruct((rows // 32, LANES), jnp.float32),
+        in_specs=[pl.BlockSpec(memory_space=pltpu.SMEM)] + [vmem] * len(parts) + [hbm, hbm],
         out_specs=vmem,
-        scratch_shapes=[pltpu.VMEM((n * rows, 2 * cols), jnp.float32)],
+        scratch_shapes=[
+            pltpu.VMEM((rows, 2 * cols), jnp.float32),
+            pltpu.VMEM((2 * cols // TILE, width, TILE), jnp.bfloat16),
+            pltpu.SemaphoreType.DMA((2 * cols // TILE,)),
+        ],
         cost_estimate=pl.CostEstimate(
-            flops=4 * n * rows * width * cols, bytes_accessed=n * rows * width * 2, transcendentals=2 * n * rows * cols
+            flops=4 * rows * width * cols, bytes_accessed=4 * width * cols, transcendentals=2 * rows * cols
         ),
-        compiler_params=pltpu.CompilerParams(vmem_limit_bytes=16 << 20),
+        compiler_params=pltpu.CompilerParams(vmem_limit_bytes=22 << 20),
         name="score",
     )(bases, *parts, w_own, w_other)
 
@@ -139,7 +158,7 @@
             out_ref[pl.ds(o * copies + c, 1), :] = row
         return carry
 
-    lax.fori_loop(0, table.shape[0], deal, 0)
+    lax.fori_loop(0, table.shape[0], deal, 0, unroll=8)
 
 
 def deal_lines(place, owner, lines, copies):
@@ -189,53 +208,55 @@
     )(lengths, lines)
 
 
-def places():
-    zl, x, core = lax.axis_index("zl"), lax.axis_index("x"), lax.axis_index("core")
-    outer, inner = jnp.where(core == 0, zl, x), jnp.where(core == 0, x, zl)
-
-    def line(step, offset, halves):
-        far, near = (outer + step) % 4, (inner + offset) % 4
-        z, col = jnp.where(core == 0, far, near), jnp.where(core == 0, near, far)
-        return [((half * 4 + z) * 4 + col) * 2 + core for half in halves]
-
-    both = (0, 1)
+PLACES, SPOTS = 32, 6
+
+
+def guide():
+    table = np.zeros((8, 4, 2, 4, PLACES + SPOTS + 2), np.int32)
     order = [(0, o) for o in (0, 3, 1, 2)] + [(3, 0), (3, 3), (1, 0), (1, 3)]
     order += [(3, 1), (3, 2), (1, 1), (1, 2), (2, 0), (2, 3), (2, 1), (2, 2)]
-    return jnp.stack([w for step, offset in order for w in line(step, offset, both)]).astype(jnp.int32)
+    for z, x, core, tp in np.ndindex(8, 4, 2, 4):
+        outer, inner = (z % 4, x) if core == 0 else (x, z % 4)
+        row = []
+        for step, offset in order:
+            far, near = (outer + step) % 4, (inner + offset) % 4
+            at_z, at_x = (far, near) if core == 0 else (near, far)
+            row += [((half * 4 + at_z) * 4 + at_x) * 2 + core for half in range(2)]
+        row += [z // 4, 1 - z // 4] + [(tp + k) % 4 for k in (0, 1, 3, 2)]
+        row += [((z * 4 + x) * 2 + c) * 4 + tp for c in (core, 1 - core)]
+        table[z, x, core, tp] = row
+    return jnp.asarray(table.reshape(256, -1))
 
 
 def local(hidden, gain, head_weight, token_ids, lengths, owner_device):
-    core = lax.axis_index("core")
-    cols, slots = head_weight.shape[1], hidden.shape[0]
+    slots = hidden.shape[0]
+    device = lax.axis_index(ALL)
+    index = lax.dynamic_index_in_dim(guide(), device, 0, keepdims=False)
     other_weight = lax.ppermute(head_weight, "core", [(0, 1), (1, 0)])
-    chip = ((lax.axis_index("zh") * 4 + lax.axis_index("zl")) * 4 + lax.axis_index("x")) * 2
-    base = lambda c: ((chip + c) * 4 + lax.axis_index("tp")) * cols
-    bases = jnp.stack([base(core), base(1 - core)]).astype(jnp.int32)
 
     ids = token_ids[:, None]
     lane = lax.broadcasted_iota(jnp.int32, (slots, LANES), 1)
     digits = jnp.where(lane == 0, ids >> 12, jnp.where(lane == 1, (ids >> 6) & 63, jnp.where(lane == 2, ids & 63, 0)))
     block = jnp.concatenate([hidden, digits.astype(jnp.bfloat16)], axis=1)
+    block, index = lax.optimization_barrier((block, index))
     partner = lax.ppermute(block, "zh", [(0, 1), (1, 0)])
     around = lambda value: [value] + [lax.ppermute(value, "tp", [(i, (i - k) % 4) for i in range(4)]) for k in (1, 3, 2)]
-    half, quarter = lax.axis_index("zh"), lax.axis_index("tp")
-    spots = jnp.stack([half, 1 - half] + [(quarter + k) % 4 for k in (0, 1, 3, 2)]).astype(jnp.int32)
-    own = norm(spots, around(block) + around(partner), gain)
+    own = norm(index, around(block) + around(partner), gain)
     own, other_weight = lax.optimization_barrier((own, other_weight))
 
     both = (head_weight, other_weight)
-    lines = ring(own, both, bases, slots)
-    dealt = deal_lines(places(), owner_device, lines, 4)
+    lines = ring(own, both, index, slots)
+    dealt = deal_lines(index, owner_device, lines, 4)
     met = lax.all_to_all(dealt, ALL, 0, 0, tiled=True)
     return merge(lengths, met, slots)
 
 
-def ring(own, both, bases, slots):
+def ring(own, both, index, slots):
     def move(value, step, swap=False):
         return send(value, step, swap)
 
     def scored(parts):
-        return score(parts, *both, bases)
+        return score(parts, *both, index)
 
     f1, b1 = move(own, 1, True), move(own, -1, True)
     first = jnp.concatenate([own, f1], axis=0)
@@ -246,7 +267,7 @@
     rows = slots * 2
     fc, bc = move(fa[:rows], 1), move(ba[rows:], -1)
     fd, bd = move(fb[:rows], 1), move(bb[rows:], -1)
-    return [scored([first, second]), scored([fa, ba]), scored([fb, bb]), scored([fc, bc]), scored([fd, bd])]
+    return [scored([first, second, fa, ba]), scored([fb, bb, fc, bc]), scored([fd, bd])]
 
 
 def solution(mesh):

time: 144 us -> 129 us (0.90)
  Pallas kernels: 38.6 us -> 26.3 us
  local copies, waits for them, and re-layouts: 7.66 us -> 1.89 us
  waiting for transfers between devices: 47.3 us -> 51 us
    pallas_call x5 -> x3, Pallas kernels: 35.4 us -> 23.4 us  [score(): pl.pallas_call(functools.partial(score_kernel, sizes, width), out_shape=j...]
    ppermute x12, waiting for transfers between devices: 29.9 us -> 33.5 us  [send(): return lax.ppermute(value, REQ, pairs(step, swap))]
    unnamed x9 -> x11, local copies, waits for them, and re-layouts: 3.35 us -> 0.87 us
    slice x2, local copies, waits for them, and re-layouts: 2.28 us -> 0.09 us  [ring(): fd, bd = (move(fb[:rows], 1), move(bb[rows:], -1))]
  transfers between devices with their start and end apart: 21 -> 21, of which waited for: 9 -> 9; matrix products, arithmetic and copies ran while one was open for 6% -> 2% of each run, Pallas kernels for 21% -> 15%
where the time goes in v1:
time: 129 us; the launch traced here: 128 us
  waiting for transfers between devices  51 us (40%)
  starting transfers between devices  45.9 us (36%)
  Pallas kernels  26.3 us (20%)
  local copies, waits for them, and re-layouts  1.89 us (1%)
  other arithmetic  1.65 us (1%)
  between operations  1.47 us (1%)
    ppermute x12, waiting for transfers between devices, send(): return lax.ppermute(value, REQ, pairs(step, swap))  33.5 us
    pallas_call x3, Pallas kernels, score(): pl.pallas_call(functools.partial(score_kernel, sizes, width), out_shape=j...  23.4 us
    ppermute x12, starting transfers between devices, send(): return lax.ppermute(value, REQ, pairs(step, swap))  18.4 us
    all_to_all x1, waiting for transfers between devices, local(): met = lax.all_to_all(dealt, ALL, 0, 0, tiled=True)  12.1 us
    all_to_all x1, starting transfers between devices, local(): met = lax.all_to_all(dealt, ALL, 0, 0, tiled=True)  11.3 us
    ppermute x6, starting transfers between devices, local(): lax.ppermute(value, 'tp', [(i, (i - k) % 4) for i in range(4)])  7.69 us
    ppermute x6, waiting for transfers between devices, local(): lax.ppermute(value, 'tp', [(i, (i - k) % 4) for i in range(4)])  5.45 us
    ppermute x1, starting transfers between devices, local(): partner = lax.ppermute(block, 'zh', [(0, 1), (1, 0)])  5.2 us
  transfers between devices with their start and end apart: 21, of which 9 were waited for; matrix products, arithmetic and copies ran while one was open for 2% of the time, Pallas kernels for 15%

profile of v1, /device:TPU:1, one launch (start us, length us, event | category | flops | bytes accessed | tf_op | source)
XLA Modules:
  0.0 128.3 jit_solution(9043716761533586274)
XLA Ops:
  0.6 3.3 %collective-permute-start.7 = (bf16[5120,512]{1,0:T(8,128)(2,1)}, bf16[5120,512]{1,0:T(8,128)(2,1)}, u32[]{:S(2)}, u32[]{:S(2)}) collective-permute-start(bf16[5120,512]{1,0:T(8,128)(2,1)} %refs_2_.1), channel_id=1, source_target_pairs={{0,4},{4,0},{1,5},{5,1},{2,6},{6,2},{3,7},{7,3},{8,12},{12,8},{9,1... | collective-permute-start | bytes 15728648 | tf_op jit(solution)/shard_map/ppermute | solution.py:235
  3.9 0.7 dynamic-slice_bitcast_fusion.spot_ref.base_ref.place_ref
  4.6 0.7 broadcast_shift-right-arithmetic_fusion
  5.3 0.1 select_convert_fusion
  5.4 0.9 pad_maximum_fusion.refs_0_
  6.3 5.2 %collective-permute-start.3 = (bf16[32,1408]{1,0:T(8,128)(2,1)S(1)}, bf16[32,1408]{1,0:T(8,128)(2,1)S(1)}, u32[]{:S(2)}, u32[]{:S(2)}) collective-permute-start(bf16[32,1408]{1,0:T(8,128)(2,1)S(1)} %pad_maximum_fusion.refs_0_), channel_id=1, source_target_pairs={{0,128},{128,0},{1,129},{129,1},{2,130},{130,2},{3,131},{131,3},{4... | collective-permute-start | bytes 270344 | tf_op jit(solution)/shard_map/ppermute | solution.py:242
  11.5 2.9 %collective-permute-start.2 = (bf16[32,1408]{1,0:T(8,128)(2,1)S(1)}, bf16[32,1408]{1,0:T(8,128)(2,1)S(1)}, u32[]{:S(2)}, u32[]{:S(2)}) collective-permute-start(bf16[32,1408]{1,0:T(8,128)(2,1)S(1)} %pad_maximum_fusion.refs_0_), channel_id=1, source_target_pairs={{0,2},{1,3},{2,0},{3,1},{4,6},{5,7},{6,4},{7,5},{8,10},{9,11},{10,... | collective-permute-start | bytes 270344 | tf_op jit(solution)/shard_map/ppermute | solution.py:243
  14.4 0.4 collective-permute-start.1
  14.8 2.3 %collective-permute-start = (bf16[32,1408]{1,0:T(8,128)(2,1)S(1)}, bf16[32,1408]{1,0:T(8,128)(2,1)S(1)}, u32[]{:S(2)}, u32[]{:S(2)}) collective-permute-start(bf16[32,1408]{1,0:T(8,128)(2,1)S(1)} %pad_maximum_fusion.refs_0_), channel_id=1, source_target_pairs={{0,3},{1,0},{2,1},{3,2},{4,7},{5,4},{6,5},{7,6},{8,11},{9,8},{10,9... | collective-permute-start | bytes 270344 | tf_op jit(solution)/shard_map/ppermute | solution.py:243
  17.1 0.0 collective-permute-done.3.refs_4_
  17.1 0.3 collective-permute-start.6
  17.3 0.0 collective-permute-done.2.refs_3_
  17.3 0.8 collective-permute-start.5
  18.1 0.8 collective-permute-done.1.refs_2_
  19.0 1.0 collective-permute-start.4
  20.0 0.0 collective-permute-done.refs_1_
  20.0 2.0 %collective-permute-done.6.refs_7_ = bf16[32,1408]{1,0:T(8,128)(2,1)S(1)} collective-permute-done((bf16[32,1408]{1,0:T(8,128)(2,1)S(1)}, bf16[32,1408]{1,0:T(8,128)(2,1)S(1)}, u32[]{:S(2)}, u32[]{:S(2)}) %collective-permute-start.6) | collective-permute-done | bytes 90144 | tf_op jit(solution)/shard_map/ppermute | solution.py:243
  22.0 2.6 %collective-permute-done.5.refs_6_ = bf16[32,1408]{1,0:T(8,128)(2,1)S(1)} collective-permute-done((bf16[32,1408]{1,0:T(8,128)(2,1)S(1)}, bf16[32,1408]{1,0:T(8,128)(2,1)S(1)}, u32[]{:S(2)}, u32[]{:S(2)}) %collective-permute-start.5) | collective-permute-done | bytes 90144 | tf_op jit(solution)/shard_map/ppermute | solution.py:243
  24.6 0.0 collective-permute-done.4.refs_5_
  24.6 0.0 copy-start
  24.6 0.7 copy-done
  25.3 0.0 slice-start
  25.3 0.9 norm.1
  26.2 0.0 collective-permute-done.7.refs_5_.refs_3_
  26.2 2.3 %collective-permute-start.9 = (bf16[64,5248]{1,0:T(8,128)(2,1)S(1)}, bf16[64,5248]{1,0:T(8,128)(2,1)S(1)}, u32[]{:S(2)}, u32[]{:S(2)}) collective-permute-start(bf16[64,5248]{1,0:T(8,128)(2,1)S(1)} %norm.1), channel_id=1, source_target_pairs={{0,24},{4,228},{8,0},{12,236},{16,8},{20,244},{24,16},{28,252},{32... | collective-permute-start | bytes 2015240 | tf_op jit(solution)/shard_map/ppermute | solution.py:32
  28.6 0.0 collective-permute-start.8
  28.6 11.1 %collective-permute-done.8 = bf16[64,5248]{1,0:T(8,128)(2,1)S(1)} collective-permute-done((bf16[64,5248]{1,0:T(8,128)(2,1)S(1)}, bf16[64,5248]{1,0:T(8,128)(2,1)S(1)}, u32[]{:S(2)}, u32[]{:S(2)}) %collective-permute-start.8) | collective-permute-done | bytes 671776 | tf_op jit(solution)/shard_map/ppermute | solution.py:32
  39.7 0.1 constant_dynamic-update-slice_fusion.refs_0_
  39.8 2.3 %collective-permute-start.13 = (bf16[128,5248]{1,0:T(8,128)(2,1)S(1)}, bf16[128,5248]{1,0:T(8,128)(2,1)S(1)}, u32[]{:S(2)}, u32[]{:S(2)}) collective-permute-start(bf16[128,5248]{1,0:T(8,128)(2,1)S(1)} %constant_dynamic-update-slice_fusion.refs_0_), channel_id=1, source_target_pairs={{0,224},{4,28},{8,232},{12,4},{16,240},{20,12},{24,248},{28,20},{3... | collective-permute-start | bytes 4030472 | tf_op jit(solution)/shard_map/ppermute | solution.py:32
  42.0 0.0 collective-permute-start.12
  42.0 0.0 collective-permute-done.9
  42.1 0.6 collective-permute-start.11
  42.7 0.0 slice-start.1
  42.7 1.0 collective-permute-start.10
  43.8 6.7 %collective-permute-done.10 = bf16[32,5248]{1,0:T(8,128)(2,1)S(1)} collective-permute-done((bf16[32,5248]{1,0:T(8,128)(2,1)S(1)}, bf16[32,5248]{1,0:T(8,128)(2,1)S(1)}, u32[]{:S(2)}, u32[]{:S(2)}) %collective-permute-start.10) | collective-permute-done | bytes 335904 | tf_op jit(solution)/shard_map/ppermute | solution.py:32
  50.5 1.1 collective-permute-done.11
  51.7 5.0 %collective-permute-start.15 = (bf16[128,5248]{1,0:T(8,128)(2,1)S(1)}, bf16[128,5248]{1,0:T(8,128)(2,1)S(1)}, u32[]{:S(2)}, u32[]{:S(2)}) collective-permute-start(bf16[128,5248]{1,0:T(8,128)(2,1)S(1)} %constant_dynamic-update-slice_fusion.2.refs_1_), channel_id=1, source_target_pairs={{0,224},{4,28},{8,232},{12,4},{16,240},{20,12},{24,248},{28,20},{3... | collective-permute-start | bytes 4030472 | tf_op jit(solution)/shard_map/ppermute | solution.py:32
  56.7 0.0 collective-permute-start.14
  56.7 3.9 %collective-permute-done.13.refs_3_ = bf16[128,5248]{1,0:T(8,128)(2,1)S(1)} collective-permute-done((bf16[128,5248]{1,0:T(8,128)(2,1)S(1)}, bf16[128,5248]{1,0:T(8,128)(2,1)S(1)}, u32[]{:S(2)}, u32[]{:S(2)}) %collective-permute-start.13) | collective-permute-done | bytes 1343520 | tf_op jit(solution)/shard_map/ppermute | solution.py:32
  60.6 3.5 %collective-permute-start.17 = (bf16[64,5248]{1,0:T(8,128)(2,1)S(1)}, bf16[64,5248]{1,0:T(8,128)(2,1)S(1)}, u32[]{:S(2)}, u32[]{:S(2)}) collective-permute-start(bf16[64,5248]{1,0:T(8,128)(2,1)S(1)} %slice.27), channel_id=1, source_target_pairs={{0,224},{4,28},{8,232},{12,4},{16,240},{20,12},{24,248},{28,20},{3... | collective-permute-start | bytes 2015240 | tf_op jit(solution)/shard_map/ppermute | solution.py:32
  64.1 0.0 collective-permute-done.12.refs_2_
  64.1 0.1 collective-permute-start.16
  64.2 10.7 %collective-permute-done.15.refs_1_ = bf16[128,5248]{1,0:T(8,128)(2,1)S(1)} collective-permute-done((bf16[128,5248]{1,0:T(8,128)(2,1)S(1)}, bf16[128,5248]{1,0:T(8,128)(2,1)S(1)}, u32[]{:S(2)}, u32[]{:S(2)}) %collective-permute-start.15) | collective-permute-done | bytes 1343520 | tf_op jit(solution)/shard_map/ppermute | solution.py:32
  75.0 3.5 %collective-permute-start.19 = (bf16[64,5248]{1,0:T(8,128)(2,1)S(1)}, bf16[64,5248]{1,0:T(8,128)(2,1)S(1)}, u32[]{:S(2)}, u32[]{:S(2)}) collective-permute-start(bf16[64,5248]{1,0:T(8,128)(2,1)S(1)} %slice.29), channel_id=1, source_target_pairs={{0,224},{4,28},{8,232},{12,4},{16,240},{20,12},{24,248},{28,20},{3... | collective-permute-start | bytes 2015240 | tf_op jit(solution)/shard_map/ppermute | solution.py:32
  78.5 0.0 collective-permute-done.14.refs_0_
  78.5 0.1 collective-permute-start.18
  78.6 0.0 slice-done
  78.6 0.0 slice-done.1
  78.6 10.4 %score.3.refs_0_ = f32[16,128]{1,0:T(8,128)S(1)} custom-call(s32[40]{0:T(128)S(1)} %dynamic-slice_bitcast_fusion.spot_ref.base_ref.place_ref, bf16[128,5248]{1,0:T(8,128)(2,1)S(1)} %constant_dynamic-update-slice_fusion.refs_0_, bf16[128,5248]{1,0:T(8,128)(2,1)S(1)} %constant_dynamic-update-slice_fusion.2.refs_1_, ...), custom_call_target="tpu_custom_call" | custom-call | flops 5368709120 | bytes 10485760 | tf_op jit(solution)/shard_map/score/pallas_call | solution.py:127
  89.0 0.0 collective-permute-done.17.refs_3_
  89.1 0.0 collective-permute-done.16.refs_2_
  89.1 8.2 %score.4.refs_1_ = f32[12,128]{1,0:T(8,128)S(1)} custom-call(s32[40]{0:T(128)S(1)} %dynamic-slice_bitcast_fusion.spot_ref.base_ref.place_ref, bf16[128,5248]{1,0:T(8,128)(2,1)S(1)} %collective-permute-done.14.refs_0_, bf16[128,5248]{1,0:T(8,128)(2,1)S(1)} %collective-permute-done.15.refs_1_, bf16[64,5248]{1,0:T(8,128)(2,1)S(1)} %collective-permute-done.16.refs_2_, ...), custom_call_target="tpu_custom_call" | custom-call | flops 4026531840 | bytes 10485760 | tf_op jit(solution)/shard_map/score/pallas_call | solution.py:127
  97.3 0.0 copy-start.1
  97.3 0.0 collective-permute-done.19.refs_1_
  97.3 0.0 collective-permute-done.18.refs_0_
  97.3 4.8 %score.5.refs_2_ = f32[4,128]{1,0:T(4,128)S(1)} custom-call(s32[40]{0:T(128)S(1)} %dynamic-slice_bitcast_fusion.spot_ref.base_ref.place_ref, bf16[64,5248]{1,0:T(8,128)(2,1)S(1)} %collective-permute-done.18.refs_0_, bf16[64,5248]{1,0:T(8,128)(2,1)S(1)} %collective-permute-done.19.refs_1_, bf16[5120,512]{1,0:T(8,128)(2,1)S(1)} %bitcast.8, ...), custom_call_target="tpu_custom_call" | custom-call | flops 1342177280 | bytes 10485760 | tf_op jit(solution)/shard_map/score/pallas_call | solution.py:127
  102.1 0.0 copy-done.1
  102.1 1.3 %deal.1 = f32[256,128]{1,0:T(8,128)} custom-call(s32[40]{0:T(128)S(1)} %dynamic-slice_bitcast_fusion.spot_ref.base_ref.place_ref, s32[64]{0:T(128)S(1)} %copy-done.1, f32[16,128]{1,0:T(8,128)S(1)} %score.3.refs_0_, f32[12,128]{1,0:T(8,128)S(1)} %score.4.refs_1_, f32[4,128]{1,0:T(4,128)S(1)} %score.5.refs_2_), custom_call_target="tpu_custom_call" | custom-call | tf_op jit(solution)/shard_map/deal/pallas_call | solution.py:168
  103.5 11.3 %all-to-all-start = ((f32[256,1,128]{2,1,0:T(1,128)}), f32[256,1,128]{2,1,0:T(1,128)S(1)}, u32[]{:S(2)}, u32[]{:S(2)}) async-start(f32[256,1,128]{2,1,0:T(1,128)} %bitcast.3), calls=%async_computation | async-start | bytes 262144 | tf_op jit(solution)/shard_map/all_to_all | solution.py:250
  115.5 12.1 %all-to-all-done = f32[256,1,128]{2,1,0:T(1,128)S(1)} async-done(((f32[256,1,128]{2,1,0:T(1,128)}), f32[256,1,128]{2,1,0:T(1,128)S(1)}, u32[]{:S(2)}, u32[]{:S(2)}) %all-to-all-start) | async-done | bytes 131104 | tf_op jit(solution)/shard_map/all_to_all | solution.py:250
  127.6 0.7 merge.1
  (13 shorter events, 0.4 us)
Async XLA Ops:
  0.6 25.6 %collective-permute-start.7 = (bf16[5120,512]{1,0:T(8,128)(2,1)}, bf16[5120,512]{1,0:T(8,128)(2,1)}, u32[]{:S(2)}, u32[]{:S(2)}) collective-permute-start(bf16[5120,512]{1,0:T(8,128)(2,1)} %refs_2_.1), channel_id=1, source_target_pairs={{0,4},{4,0},{1,5},{5,1},{2,6},{6,2},{3,7},{7,3},{8,12},{12,8},{9,1... | collective-permute-start | bytes 15728648 | tf_op jit(solution)/shard_map/ppermute | solution.py:235
  6.3 10.8 %collective-permute-start.3 = (bf16[32,1408]{1,0:T(8,128)(2,1)S(1)}, bf16[32,1408]{1,0:T(8,128)(2,1)S(1)}, u32[]{:S(2)}, u32[]{:S(2)}) collective-permute-start(bf16[32,1408]{1,0:T(8,128)(2,1)S(1)} %pad_maximum_fusion.refs_0_), channel_id=1, source_target_pairs={{0,128},{128,0},{1,129},{129,1},{2,130},{130,2},{3,131},{131,3},{4... | collective-permute-start | bytes 270344 | tf_op jit(solution)/shard_map/ppermute | solution.py:242
  11.5 5.9 %collective-permute-start.2 = (bf16[32,1408]{1,0:T(8,128)(2,1)S(1)}, bf16[32,1408]{1,0:T(8,128)(2,1)S(1)}, u32[]{:S(2)}, u32[]{:S(2)}) collective-permute-start(bf16[32,1408]{1,0:T(8,128)(2,1)S(1)} %pad_maximum_fusion.refs_0_), channel_id=1, source_target_pairs={{0,2},{1,3},{2,0},{3,1},{4,6},{5,7},{6,4},{7,5},{8,10},{9,11},{10,... | collective-permute-start | bytes 270344 | tf_op jit(solution)/shard_map/ppermute | solution.py:243
  14.4 4.6 %collective-permute-start.1 = (bf16[32,1408]{1,0:T(8,128)(2,1)S(1)}, bf16[32,1408]{1,0:T(8,128)(2,1)S(1)}, u32[]{:S(2)}, u32[]{:S(2)}) collective-permute-start(bf16[32,1408]{1,0:T(8,128)(2,1)S(1)} %pad_maximum_fusion.refs_0_), channel_id=1, source_target_pairs={{0,1},{1,2},{2,3},{3,0},{4,5},{5,6},{6,7},{7,4},{8,9},{9,10},{10,1... | collective-permute-start | bytes 270344 | tf_op jit(solution)/shard_map/ppermute | solution.py:243
  14.8 5.2 %collective-permute-start = (bf16[32,1408]{1,0:T(8,128)(2,1)S(1)}, bf16[32,1408]{1,0:T(8,128)(2,1)S(1)}, u32[]{:S(2)}, u32[]{:S(2)}) collective-permute-start(bf16[32,1408]{1,0:T(8,128)(2,1)S(1)} %pad_maximum_fusion.refs_0_), channel_id=1, source_target_pairs={{0,3},{1,0},{2,1},{3,2},{4,7},{5,4},{6,5},{7,6},{8,11},{9,8},{10,9... | collective-permute-start | bytes 270344 | tf_op jit(solution)/shard_map/ppermute | solution.py:243
  17.1 5.0 %collective-permute-start.6 = (bf16[32,1408]{1,0:T(8,128)(2,1)S(1)}, bf16[32,1408]{1,0:T(8,128)(2,1)S(1)}, u32[]{:S(2)}, u32[]{:S(2)}) collective-permute-start(bf16[32,1408]{1,0:T(8,128)(2,1)S(1)} %collective-permute-done.3.refs_4_), channel_id=1, source_target_pairs={{0,2},{1,3},{2,0},{3,1},{4,6},{5,7},{6,4},{7,5},{8,10},{9,11},{10,... | collective-permute-start | bytes 270344 | tf_op jit(solution)/shard_map/ppermute | solution.py:243
  17.3 7.3 %collective-permute-start.5 = (bf16[32,1408]{1,0:T(8,128)(2,1)S(1)}, bf16[32,1408]{1,0:T(8,128)(2,1)S(1)}, u32[]{:S(2)}, u32[]{:S(2)}) collective-permute-start(bf16[32,1408]{1,0:T(8,128)(2,1)S(1)} %collective-permute-done.3.refs_4_), channel_id=1, source_target_pairs={{0,1},{1,2},{2,3},{3,0},{4,5},{5,6},{6,7},{7,4},{8,9},{9,10},{10,1... | collective-permute-start | bytes 270344 | tf_op jit(solution)/shard_map/ppermute | solution.py:243
  19.0 5.7 %collective-permute-start.4 = (bf16[32,1408]{1,0:T(8,128)(2,1)S(1)}, bf16[32,1408]{1,0:T(8,128)(2,1)S(1)}, u32[]{:S(2)}, u32[]{:S(2)}) collective-permute-start(bf16[32,1408]{1,0:T(8,128)(2,1)S(1)} %collective-permute-done.3.refs_4_), channel_id=1, source_target_pairs={{0,3},{1,0},{2,1},{3,2},{4,7},{5,4},{6,5},{7,6},{8,11},{9,8},{10,9... | collective-permute-start | bytes 270344 | tf_op jit(solution)/shard_map/ppermute | solution.py:243
  24.6 0.7 copy-start
  25.3 53.3 %slice-start = ((s8[5242880]{0:T(1024)(128)(4,1)}), s8[4194304]{0:T(1024)(128)(4,1)S(1)}, s32[]{:S(2)}) async-start(s8[5242880]{0:T(1024)(128)(4,1)} %bitcast.7), calls=%async_computation.1 | async-start | bytes 8388608
  26.2 15.8 %collective-permute-start.9 = (bf16[64,5248]{1,0:T(8,128)(2,1)S(1)}, bf16[64,5248]{1,0:T(8,128)(2,1)S(1)}, u32[]{:S(2)}, u32[]{:S(2)}) collective-permute-start(bf16[64,5248]{1,0:T(8,128)(2,1)S(1)} %norm.1), channel_id=1, source_target_pairs={{0,24},{4,228},{8,0},{12,236},{16,8},{20,244},{24,16},{28,252},{32... | collective-permute-start | bytes 2015240 | tf_op jit(solution)/shard_map/ppermute | solution.py:32
  28.6 11.1 %collective-permute-start.8 = (bf16[64,5248]{1,0:T(8,128)(2,1)S(1)}, bf16[64,5248]{1,0:T(8,128)(2,1)S(1)}, u32[]{:S(2)}, u32[]{:S(2)}) collective-permute-start(bf16[64,5248]{1,0:T(8,128)(2,1)S(1)} %norm.1), channel_id=1, source_target_pairs={{0,8},{4,36},{8,16},{12,44},{16,24},{20,52},{24,0},{28,60},{32,40}... | collective-permute-start | bytes 2015240 | tf_op jit(solution)/shard_map/ppermute | solution.py:32
  39.8 20.8 %collective-permute-start.13 = (bf16[128,5248]{1,0:T(8,128)(2,1)S(1)}, bf16[128,5248]{1,0:T(8,128)(2,1)S(1)}, u32[]{:S(2)}, u32[]{:S(2)}) collective-permute-start(bf16[128,5248]{1,0:T(8,128)(2,1)S(1)} %constant_dynamic-update-slice_fusion.refs_0_), channel_id=1, source_target_pairs={{0,224},{4,28},{8,232},{12,4},{16,240},{20,12},{24,248},{28,20},{3... | collective-permute-start | bytes 4030472 | tf_op jit(solution)/shard_map/ppermute | solution.py:32
  42.0 22.0 %collective-permute-start.12 = (bf16[128,5248]{1,0:T(8,128)(2,1)S(1)}, bf16[128,5248]{1,0:T(8,128)(2,1)S(1)}, u32[]{:S(2)}, u32[]{:S(2)}) collective-permute-start(bf16[128,5248]{1,0:T(8,128)(2,1)S(1)} %constant_dynamic-update-slice_fusion.refs_0_), channel_id=1, source_target_pairs={{0,32},{4,12},{8,40},{12,20},{16,48},{20,28},{24,56},{28,4},{32,64... | collective-permute-start | bytes 4030472 | tf_op jit(solution)/shard_map/ppermute | solution.py:32
  42.1 9.6 %collective-permute-start.11 = (bf16[32,5248]{1,0:T(8,128)(2,1)S(1)}, bf16[32,5248]{1,0:T(8,128)(2,1)S(1)}, u32[]{:S(2)}, u32[]{:S(2)}) collective-permute-start(bf16[32,5248]{1,0:T(8,128)(2,1)S(1)} %slice.25), channel_id=1, source_target_pairs={{0,24},{4,228},{8,0},{12,236},{16,8},{20,244},{24,16},{28,252},{32... | collective-permute-start | bytes 1007624 | tf_op jit(solution)/shard_map/ppermute | solution.py:32
  42.7 35.9 %slice-start.1 = ((s8[5242880]{0:T(1024)(128)(4,1)}), s8[1048576]{0:T(1024)(128)(4,1)S(1)}, s32[]{:S(2)}) async-start(s8[5242880]{0:T(1024)(128)(4,1)} %bitcast.7), calls=%async_computation.2 | async-start | bytes 2097152
  42.7 7.8 %collective-permute-start.10 = (bf16[32,5248]{1,0:T(8,128)(2,1)S(1)}, bf16[32,5248]{1,0:T(8,128)(2,1)S(1)}, u32[]{:S(2)}, u32[]{:S(2)}) collective-permute-start(bf16[32,5248]{1,0:T(8,128)(2,1)S(1)} %slice.24), channel_id=1, source_target_pairs={{0,8},{4,36},{8,16},{12,44},{16,24},{20,52},{24,0},{28,60},{32,40}... | collective-permute-start | bytes 1007624 | tf_op jit(solution)/shard_map/ppermute | solution.py:32
  51.7 23.3 %collective-permute-start.15 = (bf16[128,5248]{1,0:T(8,128)(2,1)S(1)}, bf16[128,5248]{1,0:T(8,128)(2,1)S(1)}, u32[]{:S(2)}, u32[]{:S(2)}) collective-permute-start(bf16[128,5248]{1,0:T(8,128)(2,1)S(1)} %constant_dynamic-update-slice_fusion.2.refs_1_), channel_id=1, source_target_pairs={{0,224},{4,28},{8,232},{12,4},{16,240},{20,12},{24,248},{28,20},{3... | collective-permute-start | bytes 4030472 | tf_op jit(solution)/shard_map/ppermute | solution.py:32
  56.7 21.8 %collective-permute-start.14 = (bf16[128,5248]{1,0:T(8,128)(2,1)S(1)}, bf16[128,5248]{1,0:T(8,128)(2,1)S(1)}, u32[]{:S(2)}, u32[]{:S(2)}) collective-permute-start(bf16[128,5248]{1,0:T(8,128)(2,1)S(1)} %constant_dynamic-update-slice_fusion.2.refs_1_), channel_id=1, source_target_pairs={{0,32},{4,12},{8,40},{12,20},{16,48},{20,28},{24,56},{28,4},{32,64... | collective-permute-start | bytes 4030472 | tf_op jit(solution)/shard_map/ppermute | solution.py:32
  60.6 28.4 %collective-permute-start.17 = (bf16[64,5248]{1,0:T(8,128)(2,1)S(1)}, bf16[64,5248]{1,0:T(8,128)(2,1)S(1)}, u32[]{:S(2)}, u32[]{:S(2)}) collective-permute-start(bf16[64,5248]{1,0:T(8,128)(2,1)S(1)} %slice.27), channel_id=1, source_target_pairs={{0,224},{4,28},{8,232},{12,4},{16,240},{20,12},{24,248},{28,20},{3... | collective-permute-start | bytes 2015240 | tf_op jit(solution)/shard_map/ppermute | solution.py:32
  64.1 24.9 %collective-permute-start.16 = (bf16[64,5248]{1,0:T(8,128)(2,1)S(1)}, bf16[64,5248]{1,0:T(8,128)(2,1)S(1)}, u32[]{:S(2)}, u32[]{:S(2)}) collective-permute-start(bf16[64,5248]{1,0:T(8,128)(2,1)S(1)} %slice.26), channel_id=1, source_target_pairs={{0,32},{4,12},{8,40},{12,20},{16,48},{20,28},{24,56},{28,4},{32,64... | collective-permute-start | bytes 2015240 | tf_op jit(solution)/shard_map/ppermute | solution.py:32
  75.0 22.3 %collective-permute-start.19 = (bf16[64,5248]{1,0:T(8,128)(2,1)S(1)}, bf16[64,5248]{1,0:T(8,128)(2,1)S(1)}, u32[]{:S(2)}, u32[]{:S(2)}) collective-permute-start(bf16[64,5248]{1,0:T(8,128)(2,1)S(1)} %slice.29), channel_id=1, source_target_pairs={{0,224},{4,28},{8,232},{12,4},{16,240},{20,12},{24,248},{28,20},{3... | collective-permute-start | bytes 2015240 | tf_op jit(solution)/shard_map/ppermute | solution.py:32
  78.5 18.8 %collective-permute-start.18 = (bf16[64,5248]{1,0:T(8,128)(2,1)S(1)}, bf16[64,5248]{1,0:T(8,128)(2,1)S(1)}, u32[]{:S(2)}, u32[]{:S(2)}) collective-permute-start(bf16[64,5248]{1,0:T(8,128)(2,1)S(1)} %slice.28), channel_id=1, source_target_pairs={{0,32},{4,12},{8,40},{12,20},{16,48},{20,28},{24,56},{28,4},{32,64... | collective-permute-start | bytes 2015240 | tf_op jit(solution)/shard_map/ppermute | solution.py:32
  97.3 4.9 %copy-start.1 = (s32[64]{0:T(128)S(1)}, s32[64]{0:T(128)}, u32[]{:S(2)}) copy-start(s32[64]{0:T(128)} %owner_ref.1) | copy-start | bytes 772
  103.5 24.1 %all-to-all-start = ((f32[256,1,128]{2,1,0:T(1,128)}), f32[256,1,128]{2,1,0:T(1,128)S(1)}, u32[]{:S(2)}, u32[]{:S(2)}) async-start(f32[256,1,128]{2,1,0:T(1,128)} %bitcast.3), calls=%async_computation | async-start | bytes 262144 | tf_op jit(solution)/shard_map/all_to_all | solution.py:250

commit v2 on v1

--- a/solution.py
+++ b/solution.py
@@ -34,28 +34,25 @@
 
 def norm_kernel(eps, spot_ref, *refs):
     pieces, (gain_ref, out_ref) = refs[:-2], refs[-2:]
-    width, quarters = gain_ref.shape[1] // 4, 4
-    rows = pieces[0].shape[0]
-    for h in range(2):
-        mine = pieces[h * quarters : (h + 1) * quarters]
-        at = pl.ds(pl.multiple_of(spot_ref[PLACES + h] * rows, rows), rows)
-        square = jnp.zeros((rows, 1), jnp.float32)
-        for piece in mine:
-            values = piece[:, :width].astype(jnp.float32)
-            square += jnp.sum(values * values, axis=1, keepdims=True)
-        scale = lax.rsqrt(square / (width * quarters) + eps)
-        for q, piece in enumerate(mine):
-            columns = pl.ds(pl.multiple_of(spot_ref[PLACES + 2 + q] * width, LANES), width)
-            values = piece[:, :width].astype(jnp.float32)
-            out_ref[at, columns] = (values * scale * gain_ref[:, columns]).astype(jnp.bfloat16)
-        out_ref[at, quarters * width :] = mine[0][:, width:]
+    quarters = len(pieces)
+    width = gain_ref.shape[1] // quarters
+    square = jnp.zeros((pieces[0].shape[0], 1), jnp.float32)
+    for piece in pieces:
+        values = piece[:, :width].astype(jnp.float32)
+        square += jnp.sum(values * values, axis=1, keepdims=True)
+    scale = lax.rsqrt(square / (width * quarters) + eps)
+    for q, piece in enumerate(pieces):
+        columns = pl.ds(pl.multiple_of(spot_ref[PLACES + q] * width, LANES), width)
+        values = piece[:, :width].astype(jnp.float32)
+        out_ref[:, columns] = (values * scale * gain_ref[:, columns]).astype(jnp.bfloat16)
+    out_ref[:, quarters * width :] = pieces[0][:, width:]
 
 
 def norm(spots, pieces, gain):
     vmem = pl.BlockSpec(memory_space=pltpu.VMEM)
     return pl.pallas_call(
         functools.partial(norm_kernel, 1e-05),
-        out_shape=jax.ShapeDtypeStruct((2 * pieces[0].shape[0], gain.shape[0] + LANES), jnp.bfloat16),
+        out_shape=jax.ShapeDtypeStruct((pieces[0].shape[0], gain.shape[0] + LANES), jnp.bfloat16),
         in_specs=[pl.BlockSpec(memory_space=pltpu.SMEM)] + [vmem] * (len(pieces) + 1),
         out_specs=vmem,
         compiler_params=pltpu.CompilerParams(vmem_limit_bytes=4 << 20),
@@ -208,21 +205,25 @@
     )(lengths, lines)
 
 
-PLACES, SPOTS = 32, 6
+PLACES, SPOTS = 32, 4
 
 
 def guide():
     table = np.zeros((8, 4, 2, 4, PLACES + SPOTS + 2), np.int32)
-    order = [(0, o) for o in (0, 3, 1, 2)] + [(3, 0), (3, 3), (1, 0), (1, 3)]
-    order += [(3, 1), (3, 2), (1, 1), (1, 2), (2, 0), (2, 3), (2, 1), (2, 2)]
+    steps = {0: ((0, -1), (1, 2), (4, 3), (5, 6)), 1: ((0, -1), (1, -2), (4, 3), (5, 2))}
+    hops = [(0, 0), (1, 0), (0, -1), (0, 1), (1, -1), (1, 1), (2, 0), (3, 0)]
+    hops += [(2, -1), (2, 1), (3, -1), (3, 1), (0, -2), (1, -2)]
     for z, x, core, tp in np.ndindex(8, 4, 2, 4):
-        outer, inner = (z % 4, x) if core == 0 else (x, z % 4)
         row = []
-        for step, offset in order:
-            far, near = (outer + step) % 4, (inner + offset) % 4
-            at_z, at_x = (far, near) if core == 0 else (near, far)
-            row += [((half * 4 + at_z) * 4 + at_x) * 2 + core for half in range(2)]
-        row += [z // 4, 1 - z // 4] + [(tp + k) % 4 for k in (0, 1, 3, 2)]
+        for message, hop in hops + ([(0, 2), (1, 2)] if core == 0 else [(2, 2), (3, 2)]):
+            for offset in steps[core][message]:
+                if core == 0:
+                    at_z = z + hop + (4 if message > 1 else 0)
+                    at_x = x + (offset - 4 if message > 1 else offset)
+                else:
+                    at_z, at_x = z + offset, x + hop
+                row.append(((at_z % 8) * 4 + at_x % 4) * 2 + core)
+        row += [(tp + k) % 4 for k in (0, 1, 3, 2)]
         row += [((z * 4 + x) * 2 + c) * 4 + tp for c in (core, 1 - core)]
         table[z, x, core, tp] = row
     return jnp.asarray(table.reshape(256, -1))
@@ -239,35 +240,54 @@
     digits = jnp.where(lane == 0, ids >> 12, jnp.where(lane == 1, (ids >> 6) & 63, jnp.where(lane == 2, ids & 63, 0)))
     block = jnp.concatenate([hidden, digits.astype(jnp.bfloat16)], axis=1)
     block, index = lax.optimization_barrier((block, index))
-    partner = lax.ppermute(block, "zh", [(0, 1), (1, 0)])
-    around = lambda value: [value] + [lax.ppermute(value, "tp", [(i, (i - k) % 4) for i in range(4)]) for k in (1, 3, 2)]
-    own = norm(index, around(block) + around(partner), gain)
-    own, other_weight = lax.optimization_barrier((own, other_weight))
-
-    both = (head_weight, other_weight)
-    lines = ring(own, both, index, slots)
+    lines = ring(block, gain, head_weight, other_weight, index)
     dealt = deal_lines(index, owner_device, lines, 4)
     met = lax.all_to_all(dealt, ALL, 0, 0, tiled=True)
     return merge(lengths, met, slots)
 
 
-def ring(own, both, index, slots):
+def ring(block, gain, head_weight, other_weight, index):
     def move(value, step, swap=False):
         return send(value, step, swap)
 
     def scored(parts):
-        return score(parts, *both, index)
-
+        return score(parts, head_weight, other_weight, index)
+
+    def gather(value):
+        out = [value]
+        for k in (1, 3, 2):
+            out.append(lax.ppermute(value, "tp", [(i, (i - k) % 4) for i in range(4)]))
+        return out
+
+    first_core = lax.axis_index("core") == 0
+    pick = lambda one, two: jnp.where(first_core, one, two)
+
+    around = gather(block)
+    far_block = lax.ppermute(block, "zh", [(0, 1), (1, 0)])
+    own = norm(index, around, gain)
+    own, other_weight = lax.optimization_barrier((own, other_weight))
+    head_weight, other_weight = (pltpu.with_memory_space_constraint(w, pltpu.HBM) for w in (head_weight, other_weight))
     f1, b1 = move(own, 1, True), move(own, -1, True)
-    first = jnp.concatenate([own, f1], axis=0)
-    fa, ba = move(first, 1), move(first, -1)
-    f2, b2 = move(f1[:slots], 1, True), move(b1[slots:], -1, True)
-    second = jnp.concatenate([b1, f2, b2], axis=0)
-    fb, bb = move(second, 1), move(second, -1)
-    rows = slots * 2
-    fc, bc = move(fa[:rows], 1), move(ba[rows:], -1)
-    fd, bd = move(fb[:rows], 1), move(bb[rows:], -1)
-    return [scored([first, second, fa, ba]), scored([fb, bb, fc, bc]), scored([fd, bd])]
+    beside = gather(far_block)
+    partner = norm(index, beside, gain)
+    f1p, b1p = move(partner, 1, True), move(partner, -1, True)
+
+    m1 = jnp.concatenate([own, f1], axis=0)
+    m1f, m1b = move(m1, 1), move(m1, -1)
+    f2 = move(f1, 1, True)
+    m2 = jnp.concatenate([b1, f2], axis=0)
+    m2f, m2b = move(m2, 1), move(m2, -1)
+    m3 = jnp.concatenate([partner, f1p], axis=0)
+    m3f, m3b = move(m3, 1), move(m3, -1)
+    onward = pick(*lax.optimization_barrier((b1p, b1)))
+    b2 = move(onward, -1, True)
+    m4 = jnp.concatenate([b1p, b2], axis=0)
+    m4f, m4b = move(m4, 1), move(m4, -1)
+
+    c1 = move(jnp.concatenate([m1f, m2f], axis=0), 1)
+    x1 = move(pick(m1b, m3b), -1)
+    x2 = move(pick(m2b, m4b), -1)
+    return [scored([m1, m2, m1f, m1b]), scored([m2f, m2b, m3, m4]), scored([m3f, m3b, m4f, m4b]), scored([c1, x1, x2])]
 
 
 def solution(mesh):

time: 129 us -> 159 us (1.23)
  starting transfers between devices: 45.9 us -> 58 us
  waiting for transfers between devices: 51 us -> 62 us
  Pallas kernels: 26.3 us -> 33.2 us
    ppermute x12 -> x17, waiting for transfers between devices: 33.5 us -> 42 us  [send(): return lax.ppermute(value, REQ, pairs(step, swap))]
    pallas_call x3 -> x4, Pallas kernels: 23.4 us -> 29.7 us  [score(): pl.pallas_call(functools.partial(score_kernel, sizes, width), out_shape=j...]
    ppermute x12 -> x17, starting transfers between devices: 18.4 us -> 23.6 us  [send(): return lax.ppermute(value, REQ, pairs(step, swap))]
    all_to_all x1, starting transfers between devices: 11.3 us -> 16.3 us  [local(): met = lax.all_to_all(dealt, ALL, 0, 0, tiled=True)]
    ppermute x7, waiting for transfers between devices: 5.46 us -> 7.85 us  [the longest x6 5.01 us: gather(): out.append(lax.ppermute(value, 'tp', [(i, (i - k) % 4) for i in range(4)]))]
    ppermute x7, starting transfers between devices: 12.9 us -> 14.8 us  [the longest x6 9.61 us: gather(): out.append(lax.ppermute(value, 'tp', [(i, (i - k) % 4) for i in range(4)]))]
  transfers between devices with their start and end apart: 21 -> 26, of which waited for: 9 -> 13; matrix products, arithmetic and copies ran while one was open for 2% -> 2% of each run, Pallas kernels for 15% -> 15%
where the time goes in v2:
time: 159 us
  waiting for transfers between devices  62 us (39%)
  starting transfers between devices  58 us (36%)
  Pallas kernels  33.2 us (21%)
  local copies, waits for them, and re-layouts  2.31 us (1%)
  other arithmetic  2.02 us (1%)
    ppermute x17, waiting for transfers between devices, send(): return lax.ppermute(value, REQ, pairs(step, swap))  42 us
    pallas_call x4, Pallas kernels, score(): pl.pallas_call(functools.partial(score_kernel, sizes, width), out_shape=j...  29.7 us
    ppermute x17, starting transfers between devices, send(): return lax.ppermute(value, REQ, pairs(step, swap))  23.6 us
    all_to_all x1, starting transfers between devices, local(): met = lax.all_to_all(dealt, ALL, 0, 0, tiled=True)  16.3 us
    all_to_all x1, waiting for transfers between devices, local(): met = lax.all_to_all(dealt, ALL, 0, 0, tiled=True)  12.2 us
    ppermute x6, starting transfers between devices, gather(): out.append(lax.ppermute(value, 'tp', [(i, (i - k) % 4) for i in range(4)]))  9.61 us
    ppermute x1, starting transfers between devices, ring(): far_block = lax.ppermute(block, 'zh', [(0, 1), (1, 0)])  5.2 us
    ppermute x6, waiting for transfers between devices, gather(): out.append(lax.ppermute(value, 'tp', [(i, (i - k) % 4) for i in range(4)]))  5.01 us
  transfers between devices with their start and end apart: 26, of which 13 were waited for; matrix products, arithmetic and copies ran while one was open for 2% of the time, Pallas kernels for 15%

profile of v2, /device:TPU:1, one launch (start us, length us, event | category | flops | bytes accessed | tf_op | source)
XLA Modules:
  0.0 159.1 jit_solution(18167643687385974767)
XLA Ops:
  0.6 3.3 %collective-permute-start.3 = (bf16[5120,512]{1,0:T(8,128)(2,1)}, bf16[5120,512]{1,0:T(8,128)(2,1)}, u32[]{:S(2)}, u32[]{:S(2)}) collective-permute-start(bf16[5120,512]{1,0:T(8,128)(2,1)} %refs_3_.1), channel_id=1, source_target_pairs={{0,4},{4,0},{1,5},{5,1},{2,6},{6,2},{3,7},{7,3},{8,12},{12,8},{9,1... | collective-permute-start | bytes 15728648 | tf_op jit(solution)/shard_map/ppermute | solution.py:236
  3.9 0.7 dynamic-slice_bitcast_fusion.spot_ref.base_ref.place_ref
  4.6 0.7 broadcast_shift-right-arithmetic_fusion
  5.3 0.1 select_convert_fusion
  5.4 0.9 pad_maximum_fusion.2.refs_0_
  6.3 5.2 %collective-permute-start.11 = (bf16[32,1408]{1,0:T(8,128)(2,1)S(1)}, bf16[32,1408]{1,0:T(8,128)(2,1)S(1)}, u32[]{:S(2)}, u32[]{:S(2)}) collective-permute-start(bf16[32,1408]{1,0:T(8,128)(2,1)S(1)} %pad_maximum_fusion.2.refs_0_), channel_id=1, source_target_pairs={{0,128},{128,0},{1,129},{129,1},{2,130},{130,2},{3,131},{131,3},{4... | collective-permute-start | bytes 270344 | tf_op jit(solution)/shard_map/ppermute | solution.py:266
  11.5 2.8 %collective-permute-done.11.refs_0_ = bf16[32,1408]{1,0:T(8,128)(2,1)S(1)} collective-permute-done((bf16[32,1408]{1,0:T(8,128)(2,1)S(1)}, bf16[32,1408]{1,0:T(8,128)(2,1)S(1)}, u32[]{:S(2)}, u32[]{:S(2)}) %collective-permute-start.11) | collective-permute-done | bytes 90144 | tf_op jit(solution)/shard_map/ppermute | solution.py:266
  14.3 3.0 %collective-permute-start.14 = (bf16[32,1408]{1,0:T(8,128)(2,1)S(1)}, bf16[32,1408]{1,0:T(8,128)(2,1)S(1)}, u32[]{:S(2)}, u32[]{:S(2)}) collective-permute-start(bf16[32,1408]{1,0:T(8,128)(2,1)S(1)} %collective-permute-done.11.refs_0_), channel_id=1, source_target_pairs={{0,2},{1,3},{2,0},{3,1},{4,6},{5,7},{6,4},{7,5},{8,10},{9,11},{10,... | collective-permute-start | bytes 270344 | tf_op jit(solution)/shard_map/ppermute | solution.py:259
  17.3 0.4 collective-permute-start.13
  17.7 2.3 %collective-permute-start.12 = (bf16[32,1408]{1,0:T(8,128)(2,1)S(1)}, bf16[32,1408]{1,0:T(8,128)(2,1)S(1)}, u32[]{:S(2)}, u32[]{:S(2)}) collective-permute-start(bf16[32,1408]{1,0:T(8,128)(2,1)S(1)} %collective-permute-done.11.refs_0_), channel_id=1, source_target_pairs={{0,3},{1,0},{2,1},{3,2},{4,7},{5,4},{6,5},{7,6},{8,11},{9,8},{10,9... | collective-permute-start | bytes 270344 | tf_op jit(solution)/shard_map/ppermute | solution.py:259
  20.0 0.0 collective-permute-done.14.refs_3_
  20.0 2.0 %collective-permute-done.13.refs_2_ = bf16[32,1408]{1,0:T(8,128)(2,1)S(1)} collective-permute-done((bf16[32,1408]{1,0:T(8,128)(2,1)S(1)}, bf16[32,1408]{1,0:T(8,128)(2,1)S(1)}, u32[]{:S(2)}, u32[]{:S(2)}) %collective-permute-start.13) | collective-permute-done | bytes 90144 | tf_op jit(solution)/shard_map/ppermute | solution.py:259
  22.0 0.0 collective-permute-done.12.refs_1_
  22.0 0.7 copy-done
  22.7 0.8 norm.3
  23.5 1.6 collective-permute-start.15
  25.0 1.2 collective-permute-start.2
  26.3 2.0 %collective-permute-start.1 = (bf16[32,1408]{1,0:T(8,128)(2,1)S(1)}, bf16[32,1408]{1,0:T(8,128)(2,1)S(1)}, u32[]{:S(2)}, u32[]{:S(2)}) collective-permute-start(bf16[32,1408]{1,0:T(8,128)(2,1)S(1)} %pad_maximum_fusion.2.refs_0_), channel_id=1, source_target_pairs={{0,1},{1,2},{2,3},{3,0},{4,5},{5,6},{6,7},{7,4},{8,9},{9,10},{10,1... | collective-permute-start | bytes 270344 | tf_op jit(solution)/shard_map/ppermute | solution.py:259
  28.3 0.6 collective-permute-start
  28.9 1.0 collective-permute-done.2.refs_3_
  29.9 1.3 collective-permute-done.1.refs_2_
  31.2 0.8 collective-permute-done.refs_1_
  32.0 0.7 copy-done.1
  32.7 0.8 norm.2
  33.5 3.6 %collective-permute-start.16 = (bf16[32,5248]{1,0:T(8,128)(2,1)S(1)}, bf16[32,5248]{1,0:T(8,128)(2,1)S(1)}, u32[]{:S(2)}, u32[]{:S(2)}) collective-permute-start(bf16[32,5248]{1,0:T(8,128)(2,1)S(1)} %norm.3), channel_id=1, source_target_pairs={{0,24},{4,228},{8,0},{12,236},{16,8},{20,244},{24,16},{28,252},{32... | collective-permute-start | bytes 1007624 | tf_op jit(solution)/shard_map/ppermute | solution.py:32
  37.0 0.1 pad_maximum_fusion.1.refs_2_
  37.1 2.6 %collective-permute-start.19 = (bf16[64,5248]{1,0:T(8,128)(2,1)S(1)}, bf16[64,5248]{1,0:T(8,128)(2,1)S(1)}, u32[]{:S(2)}, u32[]{:S(2)}) collective-permute-start(bf16[64,5248]{1,0:T(8,128)(2,1)S(1)} %pad_maximum_fusion.1.refs_2_), channel_id=1, source_target_pairs={{0,224},{4,28},{8,232},{12,4},{16,240},{20,12},{24,248},{28,20},{3... | collective-permute-start | bytes 2015240 | tf_op jit(solution)/shard_map/ppermute | solution.py:32
  39.7 0.0 collective-permute-start.18
  39.7 1.5 collective-permute-done.16
  41.2 0.0 collective-permute-done.3.refs_5_.refs_4_
  41.2 3.2 %collective-permute-start.5 = (bf16[32,5248]{1,0:T(8,128)(2,1)S(1)}, bf16[32,5248]{1,0:T(8,128)(2,1)S(1)}, u32[]{:S(2)}, u32[]{:S(2)}) collective-permute-start(bf16[32,5248]{1,0:T(8,128)(2,1)S(1)} %norm.2), channel_id=1, source_target_pairs={{0,24},{4,228},{8,0},{12,236},{16,8},{20,244},{24,16},{28,252},{32... | collective-permute-start | bytes 1007624 | tf_op jit(solution)/shard_map/ppermute | solution.py:32
  44.4 10.7 %collective-permute-done.4 = bf16[32,5248]{1,0:T(8,128)(2,1)S(1)} collective-permute-done((bf16[32,5248]{1,0:T(8,128)(2,1)S(1)}, bf16[32,5248]{1,0:T(8,128)(2,1)S(1)}, u32[]{:S(2)}, u32[]{:S(2)}) %collective-permute-start.4) | collective-permute-done | bytes 335904 | tf_op jit(solution)/shard_map/ppermute | solution.py:32
  55.2 2.9 %collective-permute-start.8 = (bf16[64,5248]{1,0:T(8,128)(2,1)S(1)}, bf16[64,5248]{1,0:T(8,128)(2,1)S(1)}, u32[]{:S(2)}, u32[]{:S(2)}) collective-permute-start(bf16[64,5248]{1,0:T(8,128)(2,1)S(1)} %constant_dynamic-update-slice_fusion.refs_0_), channel_id=1, source_target_pairs={{0,224},{4,28},{8,232},{12,4},{16,240},{20,12},{24,248},{28,20},{3... | collective-permute-start | bytes 2015240 | tf_op jit(solution)/shard_map/ppermute | solution.py:32
  58.1 0.0 collective-permute-done.5
  58.1 0.3 collective-permute-start.6
  58.4 7.2 %collective-permute-done.6 = bf16[32,5248]{1,0:T(8,128)(2,1)S(1)} collective-permute-done((bf16[32,5248]{1,0:T(8,128)(2,1)S(1)}, bf16[32,5248]{1,0:T(8,128)(2,1)S(1)}, u32[]{:S(2)}, u32[]{:S(2)}) %collective-permute-start.6) | collective-permute-done | bytes 335904 | tf_op jit(solution)/shard_map/ppermute | solution.py:32
  65.6 0.0 collective-permute-start.17
  65.7 8.3 %collective-permute-done.17 = bf16[32,5248]{1,0:T(8,128)(2,1)S(1)} collective-permute-done((bf16[32,5248]{1,0:T(8,128)(2,1)S(1)}, bf16[32,5248]{1,0:T(8,128)(2,1)S(1)}, u32[]{:S(2)}, u32[]{:S(2)}) %collective-permute-start.17) | collective-permute-done | bytes 335904 | tf_op jit(solution)/shard_map/ppermute | solution.py:32
  73.9 2.1 %collective-permute-start.10 = (bf16[64,5248]{1,0:T(8,128)(2,1)S(1)}, bf16[64,5248]{1,0:T(8,128)(2,1)S(1)}, u32[]{:S(2)}, u32[]{:S(2)}) collective-permute-start(bf16[64,5248]{1,0:T(8,128)(2,1)S(1)} %constant_dynamic-update-slice_fusion.2.refs_1_), channel_id=1, source_target_pairs={{0,224},{4,28},{8,232},{12,4},{16,240},{20,12},{24,248},{28,20},{3... | collective-permute-start | bytes 2015240 | tf_op jit(solution)/shard_map/ppermute | solution.py:32
  76.0 0.0 collective-permute-done.19.refs_1_
  76.0 0.1 collective-permute-start.9
  76.1 2.7 %collective-permute-start.21 = (bf16[64,5248]{1,0:T(8,128)(2,1)S(1)}, bf16[64,5248]{1,0:T(8,128)(2,1)S(1)}, u32[]{:S(2)}, u32[]{:S(2)}) collective-permute-start(bf16[64,5248]{1,0:T(8,128)(2,1)S(1)} %constant_dynamic-update-slice_fusion.4.refs_3_), channel_id=1, source_target_pairs={{0,224},{4,28},{8,232},{12,4},{16,240},{20,12},{24,248},{28,20},{3... | collective-permute-start | bytes 2015240 | tf_op jit(solution)/shard_map/ppermute | solution.py:32
  78.8 0.1 broadcast_select_fusion.1
  78.9 0.1 collective-permute-start.20
  79.0 8.0 %collective-permute-done.9.refs_0_ = bf16[64,5248]{1,0:T(8,128)(2,1)S(1)} collective-permute-done((bf16[64,5248]{1,0:T(8,128)(2,1)S(1)}, bf16[64,5248]{1,0:T(8,128)(2,1)S(1)}, u32[]{:S(2)}, u32[]{:S(2)}) %collective-permute-start.9) | collective-permute-done | bytes 671776 | tf_op jit(solution)/shard_map/ppermute | solution.py:32
  86.9 0.0 collective-permute-start.23
  86.9 0.1 pad_maximum_fusion
  87.0 0.3 collective-permute-done.10.refs_1_
  87.3 1.3 collective-permute-start.22
  88.6 6.0 %collective-permute-done.21.refs_3_ = bf16[64,5248]{1,0:T(8,128)(2,1)S(1)} collective-permute-done((bf16[64,5248]{1,0:T(8,128)(2,1)S(1)}, bf16[64,5248]{1,0:T(8,128)(2,1)S(1)}, u32[]{:S(2)}, u32[]{:S(2)}) %collective-permute-start.21) | collective-permute-done | bytes 671776 | tf_op jit(solution)/shard_map/ppermute | solution.py:32
  94.6 0.1 broadcast_select_fusion
  94.8 3.4 %collective-permute-start.24 = (bf16[64,5248]{1,0:T(8,128)(2,1)S(1)}, bf16[64,5248]{1,0:T(8,128)(2,1)S(1)}, u32[]{:S(2)}, u32[]{:S(2)}) collective-permute-start(bf16[64,5248]{1,0:T(8,128)(2,1)S(1)} %broadcast_select_fusion), channel_id=1, source_target_pairs={{0,224},{4,28},{8,232},{12,4},{16,240},{20,12},{24,248},{28,20},{3... | collective-permute-start | bytes 2015240 | tf_op jit(solution)/shard_map/ppermute | solution.py:32
  98.1 7.4 %score.4.refs_0_ = f32[8,128]{1,0:T(8,128)S(1)} custom-call(s32[38]{0:T(128)S(1)} %dynamic-slice_bitcast_fusion.spot_ref.base_ref.place_ref, bf16[64,5248]{1,0:T(8,128)(2,1)S(1)} %constant_dynamic-update-slice_fusion.refs_0_, bf16[64,5248]{1,0:T(8,128)(2,1)S(1)} %constant_dynamic-update-slice_fusion.2.refs_1_, ...), custom_call_target="tpu_custom_call" | custom-call | flops 2684354560 | bytes 10485760 | tf_op jit(solution)/shard_map/score/pallas_call | solution.py:124
  105.5 7.4 %score.5.refs_1_ = f32[8,128]{1,0:T(8,128)S(1)} custom-call(s32[38]{0:T(128)S(1)} %dynamic-slice_bitcast_fusion.spot_ref.base_ref.place_ref, bf16[64,5248]{1,0:T(8,128)(2,1)S(1)} %collective-permute-done.9.refs_0_, bf16[64,5248]{1,0:T(8,128)(2,1)S(1)} %collective-permute-done.10.refs_1_, bf16[64,5248]{1,0:T(8,128)(2,1)S(1)} %pad_maximum_fusion.1.refs_2_, ...), custom_call_target="tpu_custom_call" | custom-call | flops 2684354560 | bytes 10485760 | tf_op jit(solution)/shard_map/score/pallas_call | solution.py:124
  113.0 0.0 collective-permute-done.20.refs_2_
  113.0 7.4 %score.6.refs_2_ = f32[8,128]{1,0:T(8,128)S(1)} custom-call(s32[38]{0:T(128)S(1)} %dynamic-slice_bitcast_fusion.spot_ref.base_ref.place_ref, bf16[64,5248]{1,0:T(8,128)(2,1)S(1)} %collective-permute-done.18.refs_0_, bf16[64,5248]{1,0:T(8,128)(2,1)S(1)} %collective-permute-done.19.refs_1_, bf16[64,5248]{1,0:T(8,128)(2,1)S(1)} %collective-permute-done.20.refs_2_, ...), custom_call_target="tpu_custom_call" | custom-call | flops 2684354560 | bytes 10485760 | tf_op jit(solution)/shard_map/score/pallas_call | solution.py:124
  120.4 0.0 copy-start.2
  120.4 0.0 collective-permute-done.23.refs_1_
  120.4 0.0 collective-permute-done.22.refs_0_
  120.4 7.4 %score.7.refs_3_ = f32[8,128]{1,0:T(8,128)S(1)} custom-call(s32[38]{0:T(128)S(1)} %dynamic-slice_bitcast_fusion.spot_ref.base_ref.place_ref, bf16[128,5248]{1,0:T(8,128)(2,1)S(1)} %collective-permute-done.22.refs_0_, bf16[64,5248]{1,0:T(8,128)(2,1)S(1)} %collective-permute-done.23.refs_1_, bf16[64,5248]{1,0:T(8,128)(2,1)S(1)} %collective-permute-done.24.refs_2_, ...), custom_call_target="tpu_custom_call" | custom-call | flops 2684354560 | bytes 10485760 | tf_op jit(solution)/shard_map/score/pallas_call | solution.py:124
  127.9 1.3 deal.1
  129.2 16.3 %all-to-all-start = ((f32[256,1,128]{2,1,0:T(1,128)}), f32[256,1,128]{2,1,0:T(1,128)S(1)}, u32[]{:S(2)}, u32[]{:S(2)}) async-start(f32[256,1,128]{2,1,0:T(1,128)} %bitcast.3), calls=%async_computation | async-start | bytes 262144 | tf_op jit(solution)/shard_map/all_to_all | solution.py:245
  146.2 12.2 %all-to-all-done = f32[256,1,128]{2,1,0:T(1,128)S(1)} async-done(((f32[256,1,128]{2,1,0:T(1,128)}), f32[256,1,128]{2,1,0:T(1,128)S(1)}, u32[]{:S(2)}, u32[]{:S(2)}) %all-to-all-start) | async-done | bytes 131104 | tf_op jit(solution)/shard_map/all_to_all | solution.py:245
  158.4 0.7 merge.1
  (19 shorter events, 0.2 us)
Async XLA Ops:
  0.6 40.6 %collective-permute-start.3 = (bf16[5120,512]{1,0:T(8,128)(2,1)}, bf16[5120,512]{1,0:T(8,128)(2,1)}, u32[]{:S(2)}, u32[]{:S(2)}) collective-permute-start(bf16[5120,512]{1,0:T(8,128)(2,1)} %refs_3_.1), channel_id=1, source_target_pairs={{0,4},{4,0},{1,5},{5,1},{2,6},{6,2},{3,7},{7,3},{8,12},{12,8},{9,1... | collective-permute-start | bytes 15728648 | tf_op jit(solution)/shard_map/ppermute | solution.py:236
  6.3 8.0 %collective-permute-start.11 = (bf16[32,1408]{1,0:T(8,128)(2,1)S(1)}, bf16[32,1408]{1,0:T(8,128)(2,1)S(1)}, u32[]{:S(2)}, u32[]{:S(2)}) collective-permute-start(bf16[32,1408]{1,0:T(8,128)(2,1)S(1)} %pad_maximum_fusion.2.refs_0_), channel_id=1, source_target_pairs={{0,128},{128,0},{1,129},{129,1},{2,130},{130,2},{3,131},{131,3},{4... | collective-permute-start | bytes 270344 | tf_op jit(solution)/shard_map/ppermute | solution.py:266
  14.3 5.7 %collective-permute-start.14 = (bf16[32,1408]{1,0:T(8,128)(2,1)S(1)}, bf16[32,1408]{1,0:T(8,128)(2,1)S(1)}, u32[]{:S(2)}, u32[]{:S(2)}) collective-permute-start(bf16[32,1408]{1,0:T(8,128)(2,1)S(1)} %collective-permute-done.11.refs_0_), channel_id=1, source_target_pairs={{0,2},{1,3},{2,0},{3,1},{4,6},{5,7},{6,4},{7,5},{8,10},{9,11},{10,... | collective-permute-start | bytes 270344 | tf_op jit(solution)/shard_map/ppermute | solution.py:259
  17.3 4.6 %collective-permute-start.13 = (bf16[32,1408]{1,0:T(8,128)(2,1)S(1)}, bf16[32,1408]{1,0:T(8,128)(2,1)S(1)}, u32[]{:S(2)}, u32[]{:S(2)}) collective-permute-start(bf16[32,1408]{1,0:T(8,128)(2,1)S(1)} %collective-permute-done.11.refs_0_), channel_id=1, source_target_pairs={{0,1},{1,2},{2,3},{3,0},{4,5},{5,6},{6,7},{7,4},{8,9},{9,10},{10,1... | collective-permute-start | bytes 270344 | tf_op jit(solution)/shard_map/ppermute | solution.py:259
  17.7 4.2 %collective-permute-start.12 = (bf16[32,1408]{1,0:T(8,128)(2,1)S(1)}, bf16[32,1408]{1,0:T(8,128)(2,1)S(1)}, u32[]{:S(2)}, u32[]{:S(2)}) collective-permute-start(bf16[32,1408]{1,0:T(8,128)(2,1)S(1)} %collective-permute-done.11.refs_0_), channel_id=1, source_target_pairs={{0,3},{1,0},{2,1},{3,2},{4,7},{5,4},{6,5},{7,6},{8,11},{9,8},{10,9... | collective-permute-start | bytes 270344 | tf_op jit(solution)/shard_map/ppermute | solution.py:259
  22.0 0.7 copy-start
  23.5 13.6 %collective-permute-start.15 = (bf16[32,5248]{1,0:T(8,128)(2,1)S(1)}, bf16[32,5248]{1,0:T(8,128)(2,1)S(1)}, u32[]{:S(2)}, u32[]{:S(2)}) collective-permute-start(bf16[32,5248]{1,0:T(8,128)(2,1)S(1)} %norm.3), channel_id=1, source_target_pairs={{0,8},{4,36},{8,16},{12,44},{16,24},{20,52},{24,0},{28,60},{32,40}... | collective-permute-start | bytes 1007624 | tf_op jit(solution)/shard_map/ppermute | solution.py:32
  25.0 4.9 %collective-permute-start.2 = (bf16[32,1408]{1,0:T(8,128)(2,1)S(1)}, bf16[32,1408]{1,0:T(8,128)(2,1)S(1)}, u32[]{:S(2)}, u32[]{:S(2)}) collective-permute-start(bf16[32,1408]{1,0:T(8,128)(2,1)S(1)} %pad_maximum_fusion.2.refs_0_), channel_id=1, source_target_pairs={{0,2},{1,3},{2,0},{3,1},{4,6},{5,7},{6,4},{7,5},{8,10},{9,11},{10,... | collective-permute-start | bytes 270344 | tf_op jit(solution)/shard_map/ppermute | solution.py:259
  26.3 4.9 %collective-permute-start.1 = (bf16[32,1408]{1,0:T(8,128)(2,1)S(1)}, bf16[32,1408]{1,0:T(8,128)(2,1)S(1)}, u32[]{:S(2)}, u32[]{:S(2)}) collective-permute-start(bf16[32,1408]{1,0:T(8,128)(2,1)S(1)} %pad_maximum_fusion.2.refs_0_), channel_id=1, source_target_pairs={{0,1},{1,2},{2,3},{3,0},{4,5},{5,6},{6,7},{7,4},{8,9},{9,10},{10,1... | collective-permute-start | bytes 270344 | tf_op jit(solution)/shard_map/ppermute | solution.py:259
  28.3 3.7 %collective-permute-start = (bf16[32,1408]{1,0:T(8,128)(2,1)S(1)}, bf16[32,1408]{1,0:T(8,128)(2,1)S(1)}, u32[]{:S(2)}, u32[]{:S(2)}) collective-permute-start(bf16[32,1408]{1,0:T(8,128)(2,1)S(1)} %pad_maximum_fusion.2.refs_0_), channel_id=1, source_target_pairs={{0,3},{1,0},{2,1},{3,2},{4,7},{5,4},{6,5},{7,6},{8,11},{9,8},{10,9... | collective-permute-start | bytes 270344 | tf_op jit(solution)/shard_map/ppermute | solution.py:259
  32.0 0.7 copy-start.1
  33.5 7.7 %collective-permute-start.16 = (bf16[32,5248]{1,0:T(8,128)(2,1)S(1)}, bf16[32,5248]{1,0:T(8,128)(2,1)S(1)}, u32[]{:S(2)}, u32[]{:S(2)}) collective-permute-start(bf16[32,5248]{1,0:T(8,128)(2,1)S(1)} %norm.3), channel_id=1, source_target_pairs={{0,24},{4,228},{8,0},{12,236},{16,8},{20,244},{24,16},{28,252},{32... | collective-permute-start | bytes 1007624 | tf_op jit(solution)/shard_map/ppermute | solution.py:32
  37.1 38.9 %collective-permute-start.19 = (bf16[64,5248]{1,0:T(8,128)(2,1)S(1)}, bf16[64,5248]{1,0:T(8,128)(2,1)S(1)}, u32[]{:S(2)}, u32[]{:S(2)}) collective-permute-start(bf16[64,5248]{1,0:T(8,128)(2,1)S(1)} %pad_maximum_fusion.1.refs_2_), channel_id=1, source_target_pairs={{0,224},{4,28},{8,232},{12,4},{16,240},{20,12},{24,248},{28,20},{3... | collective-permute-start | bytes 2015240 | tf_op jit(solution)/shard_map/ppermute | solution.py:32
  39.7 73.3 %collective-permute-start.18 = (bf16[64,5248]{1,0:T(8,128)(2,1)S(1)}, bf16[64,5248]{1,0:T(8,128)(2,1)S(1)}, u32[]{:S(2)}, u32[]{:S(2)}) collective-permute-start(bf16[64,5248]{1,0:T(8,128)(2,1)S(1)} %pad_maximum_fusion.1.refs_2_), channel_id=1, source_target_pairs={{0,32},{4,12},{8,40},{12,20},{16,48},{20,28},{24,56},{28,4},{32,64... | collective-permute-start | bytes 2015240 | tf_op jit(solution)/shard_map/ppermute | solution.py:32
  41.2 16.9 %collective-permute-start.5 = (bf16[32,5248]{1,0:T(8,128)(2,1)S(1)}, bf16[32,5248]{1,0:T(8,128)(2,1)S(1)}, u32[]{:S(2)}, u32[]{:S(2)}) collective-permute-start(bf16[32,5248]{1,0:T(8,128)(2,1)S(1)} %norm.2), channel_id=1, source_target_pairs={{0,24},{4,228},{8,0},{12,236},{16,8},{20,244},{24,16},{28,252},{32... | collective-permute-start | bytes 1007624 | tf_op jit(solution)/shard_map/ppermute | solution.py:32
  44.4 10.8 %collective-permute-start.4 = (bf16[32,5248]{1,0:T(8,128)(2,1)S(1)}, bf16[32,5248]{1,0:T(8,128)(2,1)S(1)}, u32[]{:S(2)}, u32[]{:S(2)}) collective-permute-start(bf16[32,5248]{1,0:T(8,128)(2,1)S(1)} %norm.2), channel_id=1, source_target_pairs={{0,8},{4,36},{8,16},{12,44},{16,24},{20,52},{24,0},{28,60},{32,40}... | collective-permute-start | bytes 1007624 | tf_op jit(solution)/shard_map/ppermute | solution.py:32
  55.2 21.0 %collective-permute-start.8 = (bf16[64,5248]{1,0:T(8,128)(2,1)S(1)}, bf16[64,5248]{1,0:T(8,128)(2,1)S(1)}, u32[]{:S(2)}, u32[]{:S(2)}) collective-permute-start(bf16[64,5248]{1,0:T(8,128)(2,1)S(1)} %constant_dynamic-update-slice_fusion.refs_0_), channel_id=1, source_target_pairs={{0,224},{4,28},{8,232},{12,4},{16,240},{20,12},{24,248},{28,20},{3... | collective-permute-start | bytes 2015240 | tf_op jit(solution)/shard_map/ppermute | solution.py:32
  58.1 20.8 %collective-permute-start.7 = (bf16[64,5248]{1,0:T(8,128)(2,1)S(1)}, bf16[64,5248]{1,0:T(8,128)(2,1)S(1)}, u32[]{:S(2)}, u32[]{:S(2)}) collective-permute-start(bf16[64,5248]{1,0:T(8,128)(2,1)S(1)} %constant_dynamic-update-slice_fusion.refs_0_), channel_id=1, source_target_pairs={{0,32},{4,12},{8,40},{12,20},{16,48},{20,28},{24,56},{28,4},{32,64... | collective-permute-start | bytes 2015240 | tf_op jit(solution)/shard_map/ppermute | solution.py:32
  58.1 7.5 %collective-permute-start.6 = (bf16[32,5248]{1,0:T(8,128)(2,1)S(1)}, bf16[32,5248]{1,0:T(8,128)(2,1)S(1)}, u32[]{:S(2)}, u32[]{:S(2)}) collective-permute-start(bf16[32,5248]{1,0:T(8,128)(2,1)S(1)} %collective-permute-done.4), channel_id=1, source_target_pairs={{0,8},{4,36},{8,16},{12,44},{16,24},{20,52},{24,0},{28,60},{32,40}... | collective-permute-start | bytes 1007624 | tf_op jit(solution)/shard_map/ppermute | solution.py:32
  65.6 8.3 %collective-permute-start.17 = (bf16[32,5248]{1,0:T(8,128)(2,1)S(1)}, bf16[32,5248]{1,0:T(8,128)(2,1)S(1)}, u32[]{:S(2)}, u32[]{:S(2)}) collective-permute-start(bf16[32,5248]{1,0:T(8,128)(2,1)S(1)} %broadcast_select_fusion.2), channel_id=1, source_target_pairs={{0,24},{4,228},{8,0},{12,236},{16,8},{20,244},{24,16},{28,252},{32... | collective-permute-start | bytes 1007624 | tf_op jit(solution)/shard_map/ppermute | solution.py:32
  73.9 13.4 %collective-permute-start.10 = (bf16[64,5248]{1,0:T(8,128)(2,1)S(1)}, bf16[64,5248]{1,0:T(8,128)(2,1)S(1)}, u32[]{:S(2)}, u32[]{:S(2)}) collective-permute-start(bf16[64,5248]{1,0:T(8,128)(2,1)S(1)} %constant_dynamic-update-slice_fusion.2.refs_1_), channel_id=1, source_target_pairs={{0,224},{4,28},{8,232},{12,4},{16,240},{20,12},{24,248},{28,20},{3... | collective-permute-start | bytes 2015240 | tf_op jit(solution)/shard_map/ppermute | solution.py:32
  76.0 10.9 %collective-permute-start.9 = (bf16[64,5248]{1,0:T(8,128)(2,1)S(1)}, bf16[64,5248]{1,0:T(8,128)(2,1)S(1)}, u32[]{:S(2)}, u32[]{:S(2)}) collective-permute-start(bf16[64,5248]{1,0:T(8,128)(2,1)S(1)} %constant_dynamic-update-slice_fusion.2.refs_1_), channel_id=1, source_target_pairs={{0,32},{4,12},{8,40},{12,20},{16,48},{20,28},{24,56},{28,4},{32,64... | collective-permute-start | bytes 2015240 | tf_op jit(solution)/shard_map/ppermute | solution.py:32
  76.1 18.5 %collective-permute-start.21 = (bf16[64,5248]{1,0:T(8,128)(2,1)S(1)}, bf16[64,5248]{1,0:T(8,128)(2,1)S(1)}, u32[]{:S(2)}, u32[]{:S(2)}) collective-permute-start(bf16[64,5248]{1,0:T(8,128)(2,1)S(1)} %constant_dynamic-update-slice_fusion.4.refs_3_), channel_id=1, source_target_pairs={{0,224},{4,28},{8,232},{12,4},{16,240},{20,12},{24,248},{28,20},{3... | collective-permute-start | bytes 2015240 | tf_op jit(solution)/shard_map/ppermute | solution.py:32
  78.9 34.1 %collective-permute-start.20 = (bf16[64,5248]{1,0:T(8,128)(2,1)S(1)}, bf16[64,5248]{1,0:T(8,128)(2,1)S(1)}, u32[]{:S(2)}, u32[]{:S(2)}) collective-permute-start(bf16[64,5248]{1,0:T(8,128)(2,1)S(1)} %constant_dynamic-update-slice_fusion.4.refs_3_), channel_id=1, source_target_pairs={{0,32},{4,12},{8,40},{12,20},{16,48},{20,28},{24,56},{28,4},{32,64... | collective-permute-start | bytes 2015240 | tf_op jit(solution)/shard_map/ppermute | solution.py:32
  86.9 33.5 %collective-permute-start.23 = (bf16[64,5248]{1,0:T(8,128)(2,1)S(1)}, bf16[64,5248]{1,0:T(8,128)(2,1)S(1)}, u32[]{:S(2)}, u32[]{:S(2)}) collective-permute-start(bf16[64,5248]{1,0:T(8,128)(2,1)S(1)} %broadcast_select_fusion.1), channel_id=1, source_target_pairs={{0,224},{4,28},{8,232},{12,4},{16,240},{20,12},{24,248},{28,20},{3... | collective-permute-start | bytes 2015240 | tf_op jit(solution)/shard_map/ppermute | solution.py:32
  87.3 33.1 %collective-permute-start.22 = (bf16[128,5248]{1,0:T(8,128)(2,1)S(1)}, bf16[128,5248]{1,0:T(8,128)(2,1)S(1)}, u32[]{:S(2)}, u32[]{:S(2)}) collective-permute-start(bf16[128,5248]{1,0:T(8,128)(2,1)S(1)} %pad_maximum_fusion), channel_id=1, source_target_pairs={{0,32},{4,12},{8,40},{12,20},{16,48},{20,28},{24,56},{28,4},{32,64... | collective-permute-start | bytes 4030472 | tf_op jit(solution)/shard_map/ppermute | solution.py:32
  94.8 25.7 %collective-permute-start.24 = (bf16[64,5248]{1,0:T(8,128)(2,1)S(1)}, bf16[64,5248]{1,0:T(8,128)(2,1)S(1)}, u32[]{:S(2)}, u32[]{:S(2)}) collective-permute-start(bf16[64,5248]{1,0:T(8,128)(2,1)S(1)} %broadcast_select_fusion), channel_id=1, source_target_pairs={{0,224},{4,28},{8,232},{12,4},{16,240},{20,12},{24,248},{28,20},{3... | collective-permute-start | bytes 2015240 | tf_op jit(solution)/shard_map/ppermute | solution.py:32
  120.4 7.5 %copy-start.2 = (s32[64]{0:T(128)S(1)}, s32[64]{0:T(128)}, u32[]{:S(2)}) copy-start(s32[64]{0:T(128)} %owner_ref.1) | copy-start | bytes 772
  129.2 29.1 %all-to-all-start = ((f32[256,1,128]{2,1,0:T(1,128)}), f32[256,1,128]{2,1,0:T(1,128)S(1)}, u32[]{:S(2)}, u32[]{:S(2)}) async-start(f32[256,1,128]{2,1,0:T(1,128)} %bitcast.3), calls=%async_computation | async-start | bytes 262144 | tf_op jit(solution)/shard_map/all_to_all | solution.py:245

commit v3 on v2

--- a/solution.py
+++ b/solution.py
@@ -65,27 +65,17 @@
 
 def score_kernel(sizes, width, base_ref, *refs):
     n = len(sizes)
-    parts, (w_own, w_other, out_ref, logits, weights, sems) = refs[:n], refs[n:]
+    parts, (w_own, w_other, out_ref, logits) = refs[:n], refs[n:]
     cols = w_own.shape[1]
-    per_half = cols // TILE
-
-    def fetch(half, n):
-        source = (w_own, w_other)[half].at[:, pl.ds(n * TILE, TILE)]
-        slot = half * per_half + n
-        return pltpu.make_async_copy(source, weights.at[slot], sems.at[slot])
-
-    for half in range(2):
-        for i in range(per_half):
-            fetch(half, i).start()
-
-    def column_tile(slot, carry):
-        pltpu.make_async_copy(w_own.at[:, pl.ds(0, TILE)], weights.at[slot], sems.at[slot]).wait()
-        lhs = jnp.concatenate([part[:, :width] for part in parts], axis=0)
-        product = jnp.dot(lhs, weights[slot], preferred_element_type=jnp.float32)
-        logits[:, pl.ds(pl.multiple_of(slot * TILE, TILE), TILE)] = product
-        return carry
-
-    lax.fori_loop(0, 2 * per_half, column_tile, 0)
+    for half, w in enumerate((w_own, w_other)):
+
+        def column_tile(i, carry, half=half, w=w):
+            lhs = jnp.concatenate([part[:, :width] for part in parts], axis=0)
+            product = jnp.dot(lhs, w[:, pl.ds(pl.multiple_of(i * TILE, TILE), TILE)], preferred_element_type=jnp.float32)
+            logits[:, pl.ds(pl.multiple_of(half * cols + i * TILE, TILE), TILE)] = product
+            return carry
+
+        lax.fori_loop(0, cols // TILE, column_tile, 0)
 
     lane = lax.broadcasted_iota(jnp.int32, (32, LANES), 1)
     slot = lax.broadcasted_iota(jnp.int32, (32, LANES), 0)
@@ -120,21 +110,16 @@
     rows = sum(sizes)
     width, cols = w_own.shape
     vmem = pl.BlockSpec(memory_space=pltpu.VMEM)
-    hbm = pl.BlockSpec(memory_space=pltpu.HBM)
     return pl.pallas_call(
         functools.partial(score_kernel, sizes, width),
         out_shape=jax.ShapeDtypeStruct((rows // 32, LANES), jnp.float32),
-        in_specs=[pl.BlockSpec(memory_space=pltpu.SMEM)] + [vmem] * len(parts) + [hbm, hbm],
+        in_specs=[pl.BlockSpec(memory_space=pltpu.SMEM)] + [vmem] * (len(parts) + 2),
         out_specs=vmem,
-        scratch_shapes=[
-            pltpu.VMEM((rows, 2 * cols), jnp.float32),
-            pltpu.VMEM((2 * cols // TILE, width, TILE), jnp.bfloat16),
-            pltpu.SemaphoreType.DMA((2 * cols // TILE,)),
-        ],
+        scratch_shapes=[pltpu.VMEM((rows, 2 * cols), jnp.float32)],
         cost_estimate=pl.CostEstimate(
             flops=4 * rows * width * cols, bytes_accessed=4 * width * cols, transcendentals=2 * rows * cols
         ),
-        compiler_params=pltpu.CompilerParams(vmem_limit_bytes=22 << 20),
+        compiler_params=pltpu.CompilerParams(vmem_limit_bytes=16 << 20),
         name="score",
     )(bases, *parts, w_own, w_other)
 
@@ -266,7 +251,6 @@
     far_block = lax.ppermute(block, "zh", [(0, 1), (1, 0)])
     own = norm(index, around, gain)
     own, other_weight = lax.optimization_barrier((own, other_weight))
-    head_weight, other_weight = (pltpu.with_memory_space_constraint(w, pltpu.HBM) for w in (head_weight, other_weight))
     f1, b1 = move(own, 1, True), move(own, -1, True)
     beside = gather(far_block)
     partner = norm(index, beside, gain)

time: 159 us -> 160 us (level)
  no operation moved by 1% of the time
where the time goes in v3:
time: 160 us
  waiting for transfers between devices  62 us (39%)
  starting transfers between devices  58.1 us (36%)
  Pallas kernels  33.9 us (21%)
  local copies, waits for them, and re-layouts  2.32 us (1%)
  other arithmetic  1.99 us (1%)
    ppermute x17, waiting for transfers between devices, send(): return lax.ppermute(value, REQ, pairs(step, swap))  42 us
    pallas_call x4, Pallas kernels, score(): pl.pallas_call(functools.partial(score_kernel, sizes, width), out_shape=j...  30.3 us
    ppermute x17, starting transfers between devices, send(): return lax.ppermute(value, REQ, pairs(step, swap))  23.8 us
    all_to_all x1, starting transfers between devices, local(): met = lax.all_to_all(dealt, ALL, 0, 0, tiled=True)  16.2 us
    all_to_all x1, waiting for transfers between devices, local(): met = lax.all_to_all(dealt, ALL, 0, 0, tiled=True)  12.2 us
    ppermute x6, starting transfers between devices, gather(): out.append(lax.ppermute(value, 'tp', [(i, (i - k) % 4) for i in range(4)]))  9.61 us
    ppermute x1, starting transfers between devices, ring(): far_block = lax.ppermute(block, 'zh', [(0, 1), (1, 0)])  5.2 us
    ppermute x6, waiting for transfers between devices, gather(): out.append(lax.ppermute(value, 'tp', [(i, (i - k) % 4) for i in range(4)]))  5.01 us
  transfers between devices with their start and end apart: 26, of which 13 were waited for; matrix products, arithmetic and copies ran while one was open for 2% of the time, Pallas kernels for 15%

profile of v3, /device:TPU:1, one launch (start us, length us, event | category | flops | bytes accessed | tf_op | source)
XLA Modules:
  0.0 159.9 jit_solution(2532940867293488846)
XLA Ops:
  0.6 3.3 %collective-permute-start.3 = (bf16[5120,512]{1,0:T(8,128)(2,1)}, bf16[5120,512]{1,0:T(8,128)(2,1)}, u32[]{:S(2)}, u32[]{:S(2)}) collective-permute-start(bf16[5120,512]{1,0:T(8,128)(2,1)} %refs_3_.1), channel_id=1, source_target_pairs={{0,4},{4,0},{1,5},{5,1},{2,6},{6,2},{3,7},{7,3},{8,12},{12,8},{9,1... | collective-permute-start | bytes 15728648 | tf_op jit(solution)/shard_map/ppermute | solution.py:221
  3.9 0.7 dynamic-slice_bitcast_fusion.spot_ref.base_ref.place_ref
  4.6 0.7 broadcast_shift-right-arithmetic_fusion
  5.3 0.1 select_convert_fusion
  5.4 0.9 pad_maximum_fusion.2.refs_0_
  6.3 5.2 %collective-permute-start.11 = (bf16[32,1408]{1,0:T(8,128)(2,1)S(1)}, bf16[32,1408]{1,0:T(8,128)(2,1)S(1)}, u32[]{:S(2)}, u32[]{:S(2)}) collective-permute-start(bf16[32,1408]{1,0:T(8,128)(2,1)S(1)} %pad_maximum_fusion.2.refs_0_), channel_id=1, source_target_pairs={{0,128},{128,0},{1,129},{129,1},{2,130},{130,2},{3,131},{131,3},{4... | collective-permute-start | bytes 270344 | tf_op jit(solution)/shard_map/ppermute | solution.py:251
  11.5 2.8 %collective-permute-done.11.refs_0_ = bf16[32,1408]{1,0:T(8,128)(2,1)S(1)} collective-permute-done((bf16[32,1408]{1,0:T(8,128)(2,1)S(1)}, bf16[32,1408]{1,0:T(8,128)(2,1)S(1)}, u32[]{:S(2)}, u32[]{:S(2)}) %collective-permute-start.11) | collective-permute-done | bytes 90144 | tf_op jit(solution)/shard_map/ppermute | solution.py:251
  14.3 3.0 %collective-permute-start.14 = (bf16[32,1408]{1,0:T(8,128)(2,1)S(1)}, bf16[32,1408]{1,0:T(8,128)(2,1)S(1)}, u32[]{:S(2)}, u32[]{:S(2)}) collective-permute-start(bf16[32,1408]{1,0:T(8,128)(2,1)S(1)} %collective-permute-done.11.refs_0_), channel_id=1, source_target_pairs={{0,2},{1,3},{2,0},{3,1},{4,6},{5,7},{6,4},{7,5},{8,10},{9,11},{10,... | collective-permute-start | bytes 270344 | tf_op jit(solution)/shard_map/ppermute | solution.py:244
  17.3 0.4 collective-permute-start.13
  17.7 2.3 %collective-permute-start.12 = (bf16[32,1408]{1,0:T(8,128)(2,1)S(1)}, bf16[32,1408]{1,0:T(8,128)(2,1)S(1)}, u32[]{:S(2)}, u32[]{:S(2)}) collective-permute-start(bf16[32,1408]{1,0:T(8,128)(2,1)S(1)} %collective-permute-done.11.refs_0_), channel_id=1, source_target_pairs={{0,3},{1,0},{2,1},{3,2},{4,7},{5,4},{6,5},{7,6},{8,11},{9,8},{10,9... | collective-permute-start | bytes 270344 | tf_op jit(solution)/shard_map/ppermute | solution.py:244
  20.0 2.0 %collective-permute-done.13.refs_2_ = bf16[32,1408]{1,0:T(8,128)(2,1)S(1)} collective-permute-done((bf16[32,1408]{1,0:T(8,128)(2,1)S(1)}, bf16[32,1408]{1,0:T(8,128)(2,1)S(1)}, u32[]{:S(2)}, u32[]{:S(2)}) %collective-permute-start.13) | collective-permute-done | bytes 90144 | tf_op jit(solution)/shard_map/ppermute | solution.py:244
  22.0 0.0 collective-permute-done.12.refs_1_
  22.0 0.7 copy-done.1
  22.7 0.8 norm.3
  23.5 1.6 collective-permute-start.15
  25.0 1.2 collective-permute-start.2
  26.3 2.0 %collective-permute-start.1 = (bf16[32,1408]{1,0:T(8,128)(2,1)S(1)}, bf16[32,1408]{1,0:T(8,128)(2,1)S(1)}, u32[]{:S(2)}, u32[]{:S(2)}) collective-permute-start(bf16[32,1408]{1,0:T(8,128)(2,1)S(1)} %pad_maximum_fusion.2.refs_0_), channel_id=1, source_target_pairs={{0,1},{1,2},{2,3},{3,0},{4,5},{5,6},{6,7},{7,4},{8,9},{9,10},{10,1... | collective-permute-start | bytes 270344 | tf_op jit(solution)/shard_map/ppermute | solution.py:244
  28.3 0.6 collective-permute-start
  28.9 1.0 collective-permute-done.2.refs_3_
  29.9 1.3 collective-permute-done.1.refs_2_
  31.2 0.8 collective-permute-done.refs_1_
  32.0 0.7 copy-done.2
  32.7 0.8 norm.2
  33.5 3.6 %collective-permute-start.16 = (bf16[32,5248]{1,0:T(8,128)(2,1)S(1)}, bf16[32,5248]{1,0:T(8,128)(2,1)S(1)}, u32[]{:S(2)}, u32[]{:S(2)}) collective-permute-start(bf16[32,5248]{1,0:T(8,128)(2,1)S(1)} %norm.3), channel_id=1, source_target_pairs={{0,24},{4,228},{8,0},{12,236},{16,8},{20,244},{24,16},{28,252},{32... | collective-permute-start | bytes 1007624 | tf_op jit(solution)/shard_map/ppermute | solution.py:32
  37.0 0.1 pad_maximum_fusion.1.refs_2_
  37.1 2.6 %collective-permute-start.19 = (bf16[64,5248]{1,0:T(8,128)(2,1)S(1)}, bf16[64,5248]{1,0:T(8,128)(2,1)S(1)}, u32[]{:S(2)}, u32[]{:S(2)}) collective-permute-start(bf16[64,5248]{1,0:T(8,128)(2,1)S(1)} %pad_maximum_fusion.1.refs_2_), channel_id=1, source_target_pairs={{0,224},{4,28},{8,232},{12,4},{16,240},{20,12},{24,248},{28,20},{3... | collective-permute-start | bytes 2015240 | tf_op jit(solution)/shard_map/ppermute | solution.py:32
  39.7 0.0 collective-permute-start.18
  39.7 1.5 collective-permute-done.16
  41.2 0.0 collective-permute-done.3.refs_5_.refs_4_
  41.2 3.2 %collective-permute-start.5 = (bf16[32,5248]{1,0:T(8,128)(2,1)S(1)}, bf16[32,5248]{1,0:T(8,128)(2,1)S(1)}, u32[]{:S(2)}, u32[]{:S(2)}) collective-permute-start(bf16[32,5248]{1,0:T(8,128)(2,1)S(1)} %norm.2), channel_id=1, source_target_pairs={{0,24},{4,228},{8,0},{12,236},{16,8},{20,244},{24,16},{28,252},{32... | collective-permute-start | bytes 1007624 | tf_op jit(solution)/shard_map/ppermute | solution.py:32
  44.4 10.7 %collective-permute-done.4 = bf16[32,5248]{1,0:T(8,128)(2,1)S(1)} collective-permute-done((bf16[32,5248]{1,0:T(8,128)(2,1)S(1)}, bf16[32,5248]{1,0:T(8,128)(2,1)S(1)}, u32[]{:S(2)}, u32[]{:S(2)}) %collective-permute-start.4) | collective-permute-done | bytes 335904 | tf_op jit(solution)/shard_map/ppermute | solution.py:32
  55.2 2.9 %collective-permute-start.8 = (bf16[64,5248]{1,0:T(8,128)(2,1)S(1)}, bf16[64,5248]{1,0:T(8,128)(2,1)S(1)}, u32[]{:S(2)}, u32[]{:S(2)}) collective-permute-start(bf16[64,5248]{1,0:T(8,128)(2,1)S(1)} %constant_dynamic-update-slice_fusion.refs_0_), channel_id=1, source_target_pairs={{0,224},{4,28},{8,232},{12,4},{16,240},{20,12},{24,248},{28,20},{3... | collective-permute-start | bytes 2015240 | tf_op jit(solution)/shard_map/ppermute | solution.py:32
  58.1 0.0 collective-permute-done.5
  58.1 0.1 broadcast_select_fusion.2
  58.1 0.3 collective-permute-start.6
  58.4 7.2 %collective-permute-done.6 = bf16[32,5248]{1,0:T(8,128)(2,1)S(1)} collective-permute-done((bf16[32,5248]{1,0:T(8,128)(2,1)S(1)}, bf16[32,5248]{1,0:T(8,128)(2,1)S(1)}, u32[]{:S(2)}, u32[]{:S(2)}) %collective-permute-start.6) | collective-permute-done | bytes 335904 | tf_op jit(solution)/shard_map/ppermute | solution.py:32
  65.6 0.0 collective-permute-start.17
  65.7 8.3 %collective-permute-done.17 = bf16[32,5248]{1,0:T(8,128)(2,1)S(1)} collective-permute-done((bf16[32,5248]{1,0:T(8,128)(2,1)S(1)}, bf16[32,5248]{1,0:T(8,128)(2,1)S(1)}, u32[]{:S(2)}, u32[]{:S(2)}) %collective-permute-start.17) | collective-permute-done | bytes 335904 | tf_op jit(solution)/shard_map/ppermute | solution.py:32
  73.9 2.1 %collective-permute-start.10 = (bf16[64,5248]{1,0:T(8,128)(2,1)S(1)}, bf16[64,5248]{1,0:T(8,128)(2,1)S(1)}, u32[]{:S(2)}, u32[]{:S(2)}) collective-permute-start(bf16[64,5248]{1,0:T(8,128)(2,1)S(1)} %constant_dynamic-update-slice_fusion.2.refs_1_), channel_id=1, source_target_pairs={{0,224},{4,28},{8,232},{12,4},{16,240},{20,12},{24,248},{28,20},{3... | collective-permute-start | bytes 2015240 | tf_op jit(solution)/shard_map/ppermute | solution.py:32
  76.0 0.0 collective-permute-done.19.refs_1_
  76.0 0.1 collective-permute-start.9
  76.1 0.0 collective-permute-done.8.refs_3_
  76.1 2.7 %collective-permute-start.21 = (bf16[64,5248]{1,0:T(8,128)(2,1)S(1)}, bf16[64,5248]{1,0:T(8,128)(2,1)S(1)}, u32[]{:S(2)}, u32[]{:S(2)}) collective-permute-start(bf16[64,5248]{1,0:T(8,128)(2,1)S(1)} %constant_dynamic-update-slice_fusion.4.refs_3_), channel_id=1, source_target_pairs={{0,224},{4,28},{8,232},{12,4},{16,240},{20,12},{24,248},{28,20},{3... | collective-permute-start | bytes 2015240 | tf_op jit(solution)/shard_map/ppermute | solution.py:32
  78.8 0.1 broadcast_select_fusion.1
  78.9 0.1 collective-permute-start.20
  79.0 8.0 %collective-permute-done.9.refs_0_ = bf16[64,5248]{1,0:T(8,128)(2,1)S(1)} collective-permute-done((bf16[64,5248]{1,0:T(8,128)(2,1)S(1)}, bf16[64,5248]{1,0:T(8,128)(2,1)S(1)}, u32[]{:S(2)}, u32[]{:S(2)}) %collective-permute-start.9) | collective-permute-done | bytes 671776 | tf_op jit(solution)/shard_map/ppermute | solution.py:32
  86.9 0.0 collective-permute-start.23
  87.0 0.1 pad_maximum_fusion
  87.0 0.3 collective-permute-done.10.refs_1_
  87.3 1.3 collective-permute-start.22
  88.6 6.0 %collective-permute-done.21.refs_3_ = bf16[64,5248]{1,0:T(8,128)(2,1)S(1)} collective-permute-done((bf16[64,5248]{1,0:T(8,128)(2,1)S(1)}, bf16[64,5248]{1,0:T(8,128)(2,1)S(1)}, u32[]{:S(2)}, u32[]{:S(2)}) %collective-permute-start.21) | collective-permute-done | bytes 671776 | tf_op jit(solution)/shard_map/ppermute | solution.py:32
  94.6 0.1 broadcast_select_fusion
  94.7 3.6 %collective-permute-start.24 = (bf16[64,5248]{1,0:T(8,128)(2,1)S(1)}, bf16[64,5248]{1,0:T(8,128)(2,1)S(1)}, u32[]{:S(2)}, u32[]{:S(2)}) collective-permute-start(bf16[64,5248]{1,0:T(8,128)(2,1)S(1)} %broadcast_select_fusion), channel_id=1, source_target_pairs={{0,224},{4,28},{8,232},{12,4},{16,240},{20,12},{24,248},{28,20},{3... | collective-permute-start | bytes 2015240 | tf_op jit(solution)/shard_map/ppermute | solution.py:32
  98.3 7.6 %score.4.refs_0_ = f32[8,128]{1,0:T(8,128)S(1)} custom-call(s32[38]{0:T(128)S(1)} %dynamic-slice_bitcast_fusion.spot_ref.base_ref.place_ref, bf16[64,5248]{1,0:T(8,128)(2,1)S(1)} %constant_dynamic-update-slice_fusion.refs_0_, bf16[64,5248]{1,0:T(8,128)(2,1)S(1)} %constant_dynamic-update-slice_fusion.2.refs_1_, ...), custom_call_target="tpu_custom_call" | custom-call | flops 2684354560 | bytes 10485760 | tf_op jit(solution)/shard_map/score/pallas_call | solution.py:113
  105.9 7.6 %score.5.refs_1_ = f32[8,128]{1,0:T(8,128)S(1)} custom-call(s32[38]{0:T(128)S(1)} %dynamic-slice_bitcast_fusion.spot_ref.base_ref.place_ref, bf16[64,5248]{1,0:T(8,128)(2,1)S(1)} %collective-permute-done.9.refs_0_, bf16[64,5248]{1,0:T(8,128)(2,1)S(1)} %collective-permute-done.10.refs_1_, bf16[64,5248]{1,0:T(8,128)(2,1)S(1)} %pad_maximum_fusion.1.refs_2_, ...), custom_call_target="tpu_custom_call" | custom-call | flops 2684354560 | bytes 10485760 | tf_op jit(solution)/shard_map/score/pallas_call | solution.py:113
  113.5 0.0 collective-permute-done.18.refs_0_
  113.5 7.6 %score.6.refs_2_ = f32[8,128]{1,0:T(8,128)S(1)} custom-call(s32[38]{0:T(128)S(1)} %dynamic-slice_bitcast_fusion.spot_ref.base_ref.place_ref, bf16[64,5248]{1,0:T(8,128)(2,1)S(1)} %collective-permute-done.18.refs_0_, bf16[64,5248]{1,0:T(8,128)(2,1)S(1)} %collective-permute-done.19.refs_1_, bf16[64,5248]{1,0:T(8,128)(2,1)S(1)} %collective-permute-done.20.refs_2_, ...), custom_call_target="tpu_custom_call" | custom-call | flops 2684354560 | bytes 10485760 | tf_op jit(solution)/shard_map/score/pallas_call | solution.py:113
  121.1 0.0 copy-start.3
  121.1 0.0 collective-permute-done.23.refs_1_
  121.1 7.6 %score.7.refs_3_ = f32[8,128]{1,0:T(8,128)S(1)} custom-call(s32[38]{0:T(128)S(1)} %dynamic-slice_bitcast_fusion.spot_ref.base_ref.place_ref, bf16[128,5248]{1,0:T(8,128)(2,1)S(1)} %collective-permute-done.22.refs_0_, bf16[64,5248]{1,0:T(8,128)(2,1)S(1)} %collective-permute-done.23.refs_1_, bf16[64,5248]{1,0:T(8,128)(2,1)S(1)} %collective-permute-done.24.refs_2_, ...), custom_call_target="tpu_custom_call" | custom-call | flops 2684354560 | bytes 10485760 | tf_op jit(solution)/shard_map/score/pallas_call | solution.py:113
  128.7 1.3 deal.1
  130.1 16.2 %all-to-all-start = ((f32[256,1,128]{2,1,0:T(1,128)}), f32[256,1,128]{2,1,0:T(1,128)S(1)}, u32[]{:S(2)}, u32[]{:S(2)}) async-start(f32[256,1,128]{2,1,0:T(1,128)} %bitcast.3), calls=%async_computation | async-start | bytes 262144 | tf_op jit(solution)/shard_map/all_to_all | solution.py:230
  146.9 12.2 %all-to-all-done = f32[256,1,128]{2,1,0:T(1,128)S(1)} async-done(((f32[256,1,128]{2,1,0:T(1,128)}), f32[256,1,128]{2,1,0:T(1,128)S(1)}, u32[]{:S(2)}, u32[]{:S(2)}) %all-to-all-start) | async-done | bytes 131104 | tf_op jit(solution)/shard_map/all_to_all | solution.py:230
  159.2 0.7 merge.1
  (21 shorter events, 0.2 us)
Async XLA Ops:
  0.6 40.6 %collective-permute-start.3 = (bf16[5120,512]{1,0:T(8,128)(2,1)}, bf16[5120,512]{1,0:T(8,128)(2,1)}, u32[]{:S(2)}, u32[]{:S(2)}) collective-permute-start(bf16[5120,512]{1,0:T(8,128)(2,1)} %refs_3_.1), channel_id=1, source_target_pairs={{0,4},{4,0},{1,5},{5,1},{2,6},{6,2},{3,7},{7,3},{8,12},{12,8},{9,1... | collective-permute-start | bytes 15728648 | tf_op jit(solution)/shard_map/ppermute | solution.py:221
  6.3 8.0 %collective-permute-start.11 = (bf16[32,1408]{1,0:T(8,128)(2,1)S(1)}, bf16[32,1408]{1,0:T(8,128)(2,1)S(1)}, u32[]{:S(2)}, u32[]{:S(2)}) collective-permute-start(bf16[32,1408]{1,0:T(8,128)(2,1)S(1)} %pad_maximum_fusion.2.refs_0_), channel_id=1, source_target_pairs={{0,128},{128,0},{1,129},{129,1},{2,130},{130,2},{3,131},{131,3},{4... | collective-permute-start | bytes 270344 | tf_op jit(solution)/shard_map/ppermute | solution.py:251
  14.3 5.7 %collective-permute-start.14 = (bf16[32,1408]{1,0:T(8,128)(2,1)S(1)}, bf16[32,1408]{1,0:T(8,128)(2,1)S(1)}, u32[]{:S(2)}, u32[]{:S(2)}) collective-permute-start(bf16[32,1408]{1,0:T(8,128)(2,1)S(1)} %collective-permute-done.11.refs_0_), channel_id=1, source_target_pairs={{0,2},{1,3},{2,0},{3,1},{4,6},{5,7},{6,4},{7,5},{8,10},{9,11},{10,... | collective-permute-start | bytes 270344 | tf_op jit(solution)/shard_map/ppermute | solution.py:244
  17.3 4.6 %collective-permute-start.13 = (bf16[32,1408]{1,0:T(8,128)(2,1)S(1)}, bf16[32,1408]{1,0:T(8,128)(2,1)S(1)}, u32[]{:S(2)}, u32[]{:S(2)}) collective-permute-start(bf16[32,1408]{1,0:T(8,128)(2,1)S(1)} %collective-permute-done.11.refs_0_), channel_id=1, source_target_pairs={{0,1},{1,2},{2,3},{3,0},{4,5},{5,6},{6,7},{7,4},{8,9},{9,10},{10,1... | collective-permute-start | bytes 270344 | tf_op jit(solution)/shard_map/ppermute | solution.py:244
  17.7 4.2 %collective-permute-start.12 = (bf16[32,1408]{1,0:T(8,128)(2,1)S(1)}, bf16[32,1408]{1,0:T(8,128)(2,1)S(1)}, u32[]{:S(2)}, u32[]{:S(2)}) collective-permute-start(bf16[32,1408]{1,0:T(8,128)(2,1)S(1)} %collective-permute-done.11.refs_0_), channel_id=1, source_target_pairs={{0,3},{1,0},{2,1},{3,2},{4,7},{5,4},{6,5},{7,6},{8,11},{9,8},{10,9... | collective-permute-start | bytes 270344 | tf_op jit(solution)/shard_map/ppermute | solution.py:244
  22.0 0.7 copy-start.1
  23.5 13.6 %collective-permute-start.15 = (bf16[32,5248]{1,0:T(8,128)(2,1)S(1)}, bf16[32,5248]{1,0:T(8,128)(2,1)S(1)}, u32[]{:S(2)}, u32[]{:S(2)}) collective-permute-start(bf16[32,5248]{1,0:T(8,128)(2,1)S(1)} %norm.3), channel_id=1, source_target_pairs={{0,8},{4,36},{8,16},{12,44},{16,24},{20,52},{24,0},{28,60},{32,40}... | collective-permute-start | bytes 1007624 | tf_op jit(solution)/shard_map/ppermute | solution.py:32
  25.0 4.9 %collective-permute-start.2 = (bf16[32,1408]{1,0:T(8,128)(2,1)S(1)}, bf16[32,1408]{1,0:T(8,128)(2,1)S(1)}, u32[]{:S(2)}, u32[]{:S(2)}) collective-permute-start(bf16[32,1408]{1,0:T(8,128)(2,1)S(1)} %pad_maximum_fusion.2.refs_0_), channel_id=1, source_target_pairs={{0,2},{1,3},{2,0},{3,1},{4,6},{5,7},{6,4},{7,5},{8,10},{9,11},{10,... | collective-permute-start | bytes 270344 | tf_op jit(solution)/shard_map/ppermute | solution.py:244
  26.3 4.9 %collective-permute-start.1 = (bf16[32,1408]{1,0:T(8,128)(2,1)S(1)}, bf16[32,1408]{1,0:T(8,128)(2,1)S(1)}, u32[]{:S(2)}, u32[]{:S(2)}) collective-permute-start(bf16[32,1408]{1,0:T(8,128)(2,1)S(1)} %pad_maximum_fusion.2.refs_0_), channel_id=1, source_target_pairs={{0,1},{1,2},{2,3},{3,0},{4,5},{5,6},{6,7},{7,4},{8,9},{9,10},{10,1... | collective-permute-start | bytes 270344 | tf_op jit(solution)/shard_map/ppermute | solution.py:244
  28.3 3.7 %collective-permute-start = (bf16[32,1408]{1,0:T(8,128)(2,1)S(1)}, bf16[32,1408]{1,0:T(8,128)(2,1)S(1)}, u32[]{:S(2)}, u32[]{:S(2)}) collective-permute-start(bf16[32,1408]{1,0:T(8,128)(2,1)S(1)} %pad_maximum_fusion.2.refs_0_), channel_id=1, source_target_pairs={{0,3},{1,0},{2,1},{3,2},{4,7},{5,4},{6,5},{7,6},{8,11},{9,8},{10,9... | collective-permute-start | bytes 270344 | tf_op jit(solution)/shard_map/ppermute | solution.py:244
  32.0 0.7 copy-start.2
  33.5 7.7 %collective-permute-start.16 = (bf16[32,5248]{1,0:T(8,128)(2,1)S(1)}, bf16[32,5248]{1,0:T(8,128)(2,1)S(1)}, u32[]{:S(2)}, u32[]{:S(2)}) collective-permute-start(bf16[32,5248]{1,0:T(8,128)(2,1)S(1)} %norm.3), channel_id=1, source_target_pairs={{0,24},{4,228},{8,0},{12,236},{16,8},{20,244},{24,16},{28,252},{32... | collective-permute-start | bytes 1007624 | tf_op jit(solution)/shard_map/ppermute | solution.py:32
  37.1 38.9 %collective-permute-start.19 = (bf16[64,5248]{1,0:T(8,128)(2,1)S(1)}, bf16[64,5248]{1,0:T(8,128)(2,1)S(1)}, u32[]{:S(2)}, u32[]{:S(2)}) collective-permute-start(bf16[64,5248]{1,0:T(8,128)(2,1)S(1)} %pad_maximum_fusion.1.refs_2_), channel_id=1, source_target_pairs={{0,224},{4,28},{8,232},{12,4},{16,240},{20,12},{24,248},{28,20},{3... | collective-permute-start | bytes 2015240 | tf_op jit(solution)/shard_map/ppermute | solution.py:32
  39.7 73.8 %collective-permute-start.18 = (bf16[64,5248]{1,0:T(8,128)(2,1)S(1)}, bf16[64,5248]{1,0:T(8,128)(2,1)S(1)}, u32[]{:S(2)}, u32[]{:S(2)}) collective-permute-start(bf16[64,5248]{1,0:T(8,128)(2,1)S(1)} %pad_maximum_fusion.1.refs_2_), channel_id=1, source_target_pairs={{0,32},{4,12},{8,40},{12,20},{16,48},{20,28},{24,56},{28,4},{32,64... | collective-permute-start | bytes 2015240 | tf_op jit(solution)/shard_map/ppermute | solution.py:32
  41.2 16.9 %collective-permute-start.5 = (bf16[32,5248]{1,0:T(8,128)(2,1)S(1)}, bf16[32,5248]{1,0:T(8,128)(2,1)S(1)}, u32[]{:S(2)}, u32[]{:S(2)}) collective-permute-start(bf16[32,5248]{1,0:T(8,128)(2,1)S(1)} %norm.2), channel_id=1, source_target_pairs={{0,24},{4,228},{8,0},{12,236},{16,8},{20,244},{24,16},{28,252},{32... | collective-permute-start | bytes 1007624 | tf_op jit(solution)/shard_map/ppermute | solution.py:32
  44.4 10.8 %collective-permute-start.4 = (bf16[32,5248]{1,0:T(8,128)(2,1)S(1)}, bf16[32,5248]{1,0:T(8,128)(2,1)S(1)}, u32[]{:S(2)}, u32[]{:S(2)}) collective-permute-start(bf16[32,5248]{1,0:T(8,128)(2,1)S(1)} %norm.2), channel_id=1, source_target_pairs={{0,8},{4,36},{8,16},{12,44},{16,24},{20,52},{24,0},{28,60},{32,40}... | collective-permute-start | bytes 1007624 | tf_op jit(solution)/shard_map/ppermute | solution.py:32
  55.2 21.0 %collective-permute-start.8 = (bf16[64,5248]{1,0:T(8,128)(2,1)S(1)}, bf16[64,5248]{1,0:T(8,128)(2,1)S(1)}, u32[]{:S(2)}, u32[]{:S(2)}) collective-permute-start(bf16[64,5248]{1,0:T(8,128)(2,1)S(1)} %constant_dynamic-update-slice_fusion.refs_0_), channel_id=1, source_target_pairs={{0,224},{4,28},{8,232},{12,4},{16,240},{20,12},{24,248},{28,20},{3... | collective-permute-start | bytes 2015240 | tf_op jit(solution)/shard_map/ppermute | solution.py:32
  58.1 20.8 %collective-permute-start.7 = (bf16[64,5248]{1,0:T(8,128)(2,1)S(1)}, bf16[64,5248]{1,0:T(8,128)(2,1)S(1)}, u32[]{:S(2)}, u32[]{:S(2)}) collective-permute-start(bf16[64,5248]{1,0:T(8,128)(2,1)S(1)} %constant_dynamic-update-slice_fusion.refs_0_), channel_id=1, source_target_pairs={{0,32},{4,12},{8,40},{12,20},{16,48},{20,28},{24,56},{28,4},{32,64... | collective-permute-start | bytes 2015240 | tf_op jit(solution)/shard_map/ppermute | solution.py:32
  58.1 7.5 %collective-permute-start.6 = (bf16[32,5248]{1,0:T(8,128)(2,1)S(1)}, bf16[32,5248]{1,0:T(8,128)(2,1)S(1)}, u32[]{:S(2)}, u32[]{:S(2)}) collective-permute-start(bf16[32,5248]{1,0:T(8,128)(2,1)S(1)} %collective-permute-done.4), channel_id=1, source_target_pairs={{0,8},{4,36},{8,16},{12,44},{16,24},{20,52},{24,0},{28,60},{32,40}... | collective-permute-start | bytes 1007624 | tf_op jit(solution)/shard_map/ppermute | solution.py:32
  65.6 8.3 %collective-permute-start.17 = (bf16[32,5248]{1,0:T(8,128)(2,1)S(1)}, bf16[32,5248]{1,0:T(8,128)(2,1)S(1)}, u32[]{:S(2)}, u32[]{:S(2)}) collective-permute-start(bf16[32,5248]{1,0:T(8,128)(2,1)S(1)} %broadcast_select_fusion.2), channel_id=1, source_target_pairs={{0,24},{4,228},{8,0},{12,236},{16,8},{20,244},{24,16},{28,252},{32... | collective-permute-start | bytes 1007624 | tf_op jit(solution)/shard_map/ppermute | solution.py:32
  73.9 13.4 %collective-permute-start.10 = (bf16[64,5248]{1,0:T(8,128)(2,1)S(1)}, bf16[64,5248]{1,0:T(8,128)(2,1)S(1)}, u32[]{:S(2)}, u32[]{:S(2)}) collective-permute-start(bf16[64,5248]{1,0:T(8,128)(2,1)S(1)} %constant_dynamic-update-slice_fusion.2.refs_1_), channel_id=1, source_target_pairs={{0,224},{4,28},{8,232},{12,4},{16,240},{20,12},{24,248},{28,20},{3... | collective-permute-start | bytes 2015240 | tf_op jit(solution)/shard_map/ppermute | solution.py:32
  76.0 10.9 %collective-permute-start.9 = (bf16[64,5248]{1,0:T(8,128)(2,1)S(1)}, bf16[64,5248]{1,0:T(8,128)(2,1)S(1)}, u32[]{:S(2)}, u32[]{:S(2)}) collective-permute-start(bf16[64,5248]{1,0:T(8,128)(2,1)S(1)} %constant_dynamic-update-slice_fusion.2.refs_1_), channel_id=1, source_target_pairs={{0,32},{4,12},{8,40},{12,20},{16,48},{20,28},{24,56},{28,4},{32,64... | collective-permute-start | bytes 2015240 | tf_op jit(solution)/shard_map/ppermute | solution.py:32
  76.1 18.5 %collective-permute-start.21 = (bf16[64,5248]{1,0:T(8,128)(2,1)S(1)}, bf16[64,5248]{1,0:T(8,128)(2,1)S(1)}, u32[]{:S(2)}, u32[]{:S(2)}) collective-permute-start(bf16[64,5248]{1,0:T(8,128)(2,1)S(1)} %constant_dynamic-update-slice_fusion.4.refs_3_), channel_id=1, source_target_pairs={{0,224},{4,28},{8,232},{12,4},{16,240},{20,12},{24,248},{28,20},{3... | collective-permute-start | bytes 2015240 | tf_op jit(solution)/shard_map/ppermute | solution.py:32
  78.8 19.5 %copy-start = (bf16[5120,512]{1,0:T(8,128)(2,1)S(1)}, bf16[5120,512]{1,0:T(8,128)(2,1)}, u32[]{:S(2)}) copy-start(bf16[5120,512]{1,0:T(8,128)(2,1)} %refs_3_.1) | copy-start | bytes 15728644
  78.9 34.6 %collective-permute-start.20 = (bf16[64,5248]{1,0:T(8,128)(2,1)S(1)}, bf16[64,5248]{1,0:T(8,128)(2,1)S(1)}, u32[]{:S(2)}, u32[]{:S(2)}) collective-permute-start(bf16[64,5248]{1,0:T(8,128)(2,1)S(1)} %constant_dynamic-update-slice_fusion.4.refs_3_), channel_id=1, source_target_pairs={{0,32},{4,12},{8,40},{12,20},{16,48},{20,28},{24,56},{28,4},{32,64... | collective-permute-start | bytes 2015240 | tf_op jit(solution)/shard_map/ppermute | solution.py:32
  86.9 34.2 %collective-permute-start.23 = (bf16[64,5248]{1,0:T(8,128)(2,1)S(1)}, bf16[64,5248]{1,0:T(8,128)(2,1)S(1)}, u32[]{:S(2)}, u32[]{:S(2)}) collective-permute-start(bf16[64,5248]{1,0:T(8,128)(2,1)S(1)} %broadcast_select_fusion.1), channel_id=1, source_target_pairs={{0,224},{4,28},{8,232},{12,4},{16,240},{20,12},{24,248},{28,20},{3... | collective-permute-start | bytes 2015240 | tf_op jit(solution)/shard_map/ppermute | solution.py:32
  87.3 33.8 %collective-permute-start.22 = (bf16[128,5248]{1,0:T(8,128)(2,1)S(1)}, bf16[128,5248]{1,0:T(8,128)(2,1)S(1)}, u32[]{:S(2)}, u32[]{:S(2)}) collective-permute-start(bf16[128,5248]{1,0:T(8,128)(2,1)S(1)} %pad_maximum_fusion), channel_id=1, source_target_pairs={{0,32},{4,12},{8,40},{12,20},{16,48},{20,28},{24,56},{28,4},{32,64... | collective-permute-start | bytes 4030472 | tf_op jit(solution)/shard_map/ppermute | solution.py:32
  94.7 26.4 %collective-permute-start.24 = (bf16[64,5248]{1,0:T(8,128)(2,1)S(1)}, bf16[64,5248]{1,0:T(8,128)(2,1)S(1)}, u32[]{:S(2)}, u32[]{:S(2)}) collective-permute-start(bf16[64,5248]{1,0:T(8,128)(2,1)S(1)} %broadcast_select_fusion), channel_id=1, source_target_pairs={{0,224},{4,28},{8,232},{12,4},{16,240},{20,12},{24,248},{28,20},{3... | collective-permute-start | bytes 2015240 | tf_op jit(solution)/shard_map/ppermute | solution.py:32
  121.1 7.6 %copy-start.3 = (s32[64]{0:T(128)S(1)}, s32[64]{0:T(128)}, u32[]{:S(2)}) copy-start(s32[64]{0:T(128)} %owner_ref.1) | copy-start | bytes 772
  130.1 29.1 %all-to-all-start = ((f32[256,1,128]{2,1,0:T(1,128)}), f32[256,1,128]{2,1,0:T(1,128)S(1)}, u32[]{:S(2)}, u32[]{:S(2)}) async-start(f32[256,1,128]{2,1,0:T(1,128)} %bitcast.3), calls=%async_computation | async-start | bytes 262144 | tf_op jit(solution)/shard_map/all_to_all | solution.py:230
